TPU v7x, 32 devices: a whole 2x2x4 slice. The times are simulated.
32 devices in a mesh: ctx: 16 (over z, y, x), tp: 2 (over core).
Axes of the slice: x: 2, y: 2, z: 4, core: 2. Of those that a mesh axis runs over, the one named last changes fastest.
Arguments:
- tokens: bfloat16 [4096, 2688], P(('ctx', 'tp')), may hold values from -6 to 6
- result_grad: bfloat16 [4096, 2688], P(('ctx', 'tp')), may hold values from -6 to 6
- query_weight: bfloat16 [2688, 512], P(None, 'tp'), may hold values from -0.125 to 0.125
- key_weight: bfloat16 [2688, 256], P(None, 'tp'), may hold values from -0.125 to 0.125
- value_weight: bfloat16 [2688, 256], P(None, 'tp'), may hold values from -0.125 to 0.125
- output_weight: bfloat16 [512, 2688], P('tp'), may hold values from -0.5 to 0.5
- query_gain: float32 [128], replicated, may hold values from 0.5 to 1.5
- key_gain: float32 [128], replicated, may hold values from 0.5 to 1.5
Outputs:
- layer_output: bfloat16 [4096, 2688], P(('ctx', 'tp'))
- tokens_grad: bfloat16 [4096, 2688], P(('ctx', 'tp'))
All inputs are finite; a program needn't handle non-finite values.
Results may differ from a plain program's by a relative error of at most 0.012.
Values may be sent and summed in bfloat16 or wider, within the bound.
A program may use at most 64 MiB of HBM per device.

v0:
```python
import functools

import jax
import jax.numpy as jnp
import numpy as np
from jax import lax
from jax.experimental import pallas as pl
from jax.experimental.pallas import tpu as pltpu
from jax.sharding import PartitionSpec as P

WINDOW = 1024
norm_epsilon = 1e-06
score_scale = 168.0 ** (-0.5)
rope_theta = 10000.0
MESH = pl.DeviceIdType.MESH
f32 = jnp.float32
bf16 = jnp.bfloat16


def dot(a, b, ca, cb):
    return lax.dot_general(a, b, (((ca,), (cb,)), ((), ())), preferred_element_type=f32)


def rope(n, cosines, sines, half):
    return n * cosines + pltpu.roll(n, half, 1) * sines


def rope_back(g, cosines, sines, half):
    return g * cosines + pltpu.roll(g * sines, half, 1)


def inverse_rms(u):
    return lax.rsqrt(jnp.mean(u * u, axis=-1, keepdims=True) + norm_epsilon)


def norm_rope_back(g, u, gain, cosines, sines, half):
    r = inverse_rms(u)
    w = rope_back(g, cosines, sines, half) * gain
    return r * (w - u * (r * r * jnp.mean(w * u, axis=-1, keepdims=True)))


def kernel(
    n_ctx, n_tp, reach, per_kv, kv_count, head, tile,
    tokens, rgrad, qw, kw, vw, ow, qgain, kgain, freq,
    out_ref, gout_ref,
    wqkv, wo, xg, gg, raw, cos_t, sin_t, q_s, do_s, dot_s, kv_own, halo, e_s, dp_s,
    l_s, ot_s, dqt_s, att, dkv, sum4, own_grad, gin, rin, zbuf, back, part, rs_in, stage,
    local_sem, ag_send, ag_recv, f_send, f_relay, f_recv, b_send, g_recv, r_recv,
    rs_send, rs_recv, out_sem,
):
    c = lax.axis_index("ctx")
    t = lax.axis_index("tp")
    s = lax.rem(c, reach)
    z = lax.div(c, reach)
    nz = n_ctx // reach
    local, width = xg.shape[1], xg.shape[2]
    rows = local * n_tp
    half = head // 2
    qc = kv_count * per_kv * head
    kc = kv_count * head
    qn = per_kv * rows

    def local_copy(i, src, dst):
        return pltpu.make_async_copy(src, dst, local_sem.at[i])

    loads = [
        local_copy(0, tokens, xg.at[0]),
        local_copy(1, kw, wqkv.at[:, qc : qc + kc]),
        local_copy(2, vw, wqkv.at[:, qc + kc : qc + 2 * kc]),
        local_copy(3, qw, wqkv.at[:, :qc]),
        local_copy(4, rgrad, gg.at[0]),
        local_copy(5, ow, wo),
    ]
    for load in loads:
        load.start()

    def to_ctx(src, dst, send, recv, target):
        return pltpu.make_async_remote_copy(
            src_ref=src, dst_ref=dst, send_sem=send, recv_sem=recv,
            device_id={"ctx": target}, device_id_type=MESH,
        )

    def to_tp(src, dst, send, recv, target):
        return pltpu.make_async_remote_copy(
            src_ref=src, dst_ref=dst, send_sem=send, recv_sem=recv,
            device_id={"tp": target}, device_id_type=MESH,
        )

    barrier = pltpu.get_barrier_semaphore()
    for j in range(1, n_tp):
        pl.semaphore_signal(
            barrier, inc=1, device_id={"tp": lax.rem(t + j, n_tp)}, device_id_type=MESH
        )
    for j in range(1, reach):
        mate = z * reach + lax.rem(s + j, reach)
        pl.semaphore_signal(barrier, inc=1, device_id={"ctx": mate}, device_id_type=MESH)

    @pl.when(z + 1 < nz)
    def _():
        pl.semaphore_signal(barrier, inc=1, device_id={"ctx": c + reach}, device_id_type=MESH)

    @pl.when(z > 0)
    def _():
        pl.semaphore_signal(barrier, inc=1, device_id={"ctx": c - reach}, device_id_type=MESH)

    up = 2 * reach - 1 - 2 * s
    down = 2 * s + 1
    upper = (z + 1 < nz) & (up < reach)
    lower = (z > 0) & (down < reach)

    @pl.when(upper)
    def _():
        pl.semaphore_signal(barrier, inc=1, device_id={"ctx": c + up}, device_id_type=MESH)

    @pl.when(lower)
    def _():
        pl.semaphore_signal(barrier, inc=1, device_id={"ctx": c - down}, device_id_type=MESH)

    one, none = jnp.int32(1), jnp.int32(0)
    greeted = (
        n_tp - 1 + reach - 1
        + jnp.where(z > 0, one, none)
        + jnp.where(z + 1 < nz, one, none)
        + jnp.where(upper, one, none)
        + jnp.where(lower, one, none)
    )
    def place(row):
        return lax.rem(t + lax.div(row, local), n_tp) * local + lax.rem(row, local)

    row = lax.broadcasted_iota(jnp.int32, (rows, head), 0)
    angles = (c * rows + place(row)).astype(f32) * freq[...]
    lane = lax.broadcasted_iota(jnp.int32, (rows, head), 1)
    cos_t[...] = jnp.cos(angles)
    sines = jnp.sin(angles)
    sin_t[...] = jnp.where(lane < half, -sines, sines)
    pl.semaphore_wait(barrier, greeted)

    gathers = []
    for w, (src, dst) in enumerate(((tokens, xg), (rgrad, gg))):
        for j in range(1, n_tp):
            copy = to_tp(src, dst.at[n_tp - j], ag_send.at[w, j - 1], ag_recv.at[w, j - 1],
                         lax.rem(t + j, n_tp))
            copy.start()
            gathers.append((w, copy))

    spans = (slice(0, local), slice(local, rows))

    def key_values(w, x):
        span = spans[w]
        raw[span, qc : qc + 2 * kc] = dot(x, wqkv[:, qc : qc + 2 * kc], 1, 0)
        for m in range(kv_count):
            u = raw[span, qc + m * head : qc + (m + 1) * head]
            n = u * inverse_rms(u) * kgain[...]
            kv_own[0, m, span] = rope(n, cos_t[span, :], sin_t[span, :], half).astype(bf16)
            v0 = qc + kc + m * head
            kv_own[1, m, span] = raw[span, v0 : v0 + head].astype(bf16)

    def ahead(w):
        return to_ctx(kv_own.at[:, :, spans[w]], halo.at[reach - 1, :, :, spans[w]],
                      f_send.at[reach - 1, w], f_recv.at[reach - 1, w], c + reach)

    def own_to(k, w):
        return to_ctx(kv_own.at[:, :, spans[w]], halo.at[k - 1, :, :, spans[w]],
                      f_send.at[k - 1, w], f_recv.at[k - 1, w], c + k)

    def relay_to(k, w):
        return to_ctx(halo.at[reach - 1, :, :, spans[w]],
                      halo.at[reach - k - 1, :, :, spans[w]], f_relay.at[k - 1, w],
                      f_recv.at[reach - k - 1, w], c - k)

    def halo_wait(d, w):
        own_span = kv_own.at[:, :, spans[w]]
        to_ctx(own_span, halo.at[d - 1, :, :, spans[w]], f_send.at[d - 1, w],
               f_recv.at[d - 1, w], c).wait_recv()

    def sends_own(k):
        return (s + k < reach) | (upper & (up == k))

    def relays(k):
        return (k <= s) & (2 * s - k != reach - 1)

    for w in range(2):
        if w == 0:
            for i in (0, 1, 2):
                loads[i].wait()
            key_values(w, xg[0])
        else:
            for which, copy in gathers:
                if which == 0:
                    copy.wait_recv()
            key_values(w, xg[1:].reshape(rows - local, width))

        for k in range(1, reach):
            @pl.when(upper & (up == k))
            def _(k=k, w=w):
                own_to(k, w).start()

        @pl.when(z + 1 < nz)
        def _(w=w):
            ahead(w).start()

        for k in range(reach - 1, 0, -1):
            @pl.when(s + k < reach)
            def _(k=k, w=w):
                own_to(k, w).start()

    loads[3].wait()
    raw[:, :qc] = dot(xg[...].reshape(rows, width), wqkv[:, :qc], 1, 0)
    for h in range(kv_count * per_kv):
        m, g = h // per_kv, h % per_kv
        u = raw[:, h * head : (h + 1) * head]
        n = u * inverse_rms(u) * qgain[...]
        q_s[m, g * rows : (g + 1) * rows] = rope(n, cos_t[...], sin_t[...], half).astype(bf16)
    loads[4].wait()
    loads[5].wait()
    for w, copy in gathers:
        if w == 1:
            copy.wait_recv()
    d_out = dot(gg[...].reshape(rows, width), wo[...], 1, 1).astype(bf16)
    for h in range(kv_count * per_kv):
        m, g = h // per_kv, h % per_kv
        piece = d_out[:, h * head : (h + 1) * head]
        do_s[m, g * rows : (g + 1) * rows] = piece
        dot_s[m, :, g * rows : (g + 1) * rows] = piece.astype(f32).T

    def kv(d, w, m):
        return kv_own[w, m] if d == 0 else halo[d - 1, w, m]

    def first_pass(d):
        for m in range(kv_count):
            key, value = kv(d, 0, m), kv(d, 1, m)
            e = jnp.exp(dot(key, q_s[m], 1, 1) * score_scale)
            if d == 0 or d == reach:
                key_row = place(lax.broadcasted_iota(jnp.int32, (rows, 1), 0))
                query_row = place(
                    lax.rem(lax.broadcasted_iota(jnp.int32, (1, qn), 1), jnp.int32(rows))
                )
                keep = query_row >= key_row if d == 0 else query_row < key_row
                e = jnp.where(keep, e, f32(0.0))
            total = jnp.sum(e, axis=0, keepdims=True)
            low = e.astype(bf16)
            e_s[d, m] = low
            mixed = dot(value, low, 0, 0)
            dp_s[d, m] = dot(value, do_s[m], 1, 1) * score_scale
            if d == 0:
                l_s[m] = total
                ot_s[m] = mixed
            else:
                l_s[m] += total
                ot_s[m] += mixed

    first_pass(0)

    @pl.when(z > 0)
    def _():
        for w in range(2):
            halo_wait(reach, w)
            for k in range(1, reach):
                @pl.when(relays(k))
                def _(k=k, w=w):
                    relay_to(k, w).start()
        first_pass(reach)

    for d in range(1, reach):
        @pl.when(c >= d)
        def _(d=d):
            halo_wait(d, 0)
            halo_wait(d, 1)
            first_pass(d)

    inv, delta = [], []
    for m in range(kv_count):
        inv.append(1.0 / l_s[m])
        o_t = (ot_s[m] * inv[m]).astype(bf16).astype(f32)
        delta.append(jnp.sum(o_t * dot_s[m], axis=0, keepdims=True) * score_scale)
        for g in range(per_kv):
            h = m * per_kv + g
            att[:, h * head : (h + 1) * head] = o_t[:, g * rows : (g + 1) * rows].T.astype(bf16)
        l_s[m] = inv[m]
        dqt_s[m] = jnp.zeros_like(dqt_s[m])

    def second_pass(d, m):
        p = e_s[d, m].astype(f32) * inv[m]
        ds = (p * (dp_s[d, m] - delta[m])).astype(bf16)
        dk = dot(ds, q_s[m], 1, 0)
        dv = dot(p.astype(bf16), do_s[m], 1, 0)
        dqt_s[m] += dot(kv(d, 0, m), ds, 0, 0)
        return dk, dv

    def grad_home(d, w):
        return to_ctx(dkv.at[d - 1, :, :, spans[w]], gin.at[d - 1, :, :, spans[w]],
                      b_send.at[d - 1, w], g_recv.at[d - 1, w], c - d)

    def grad_mate(d, w):
        k = reach - d
        return to_ctx(dkv.at[d - 1, :, :, spans[w]], rin.at[k - 1, :, :, spans[w]],
                      b_send.at[d - 1, w], r_recv.at[k - 1, w], c + k)

    def grad_back(w):
        return to_ctx(zbuf.at[:, :, spans[w]], gin.at[reach - 1, :, :, spans[w]],
                      b_send.at[reach - 1, w], g_recv.at[reach - 1, w], c - reach)

    for d in range(reach - 1, 0, -1):
        @pl.when(c >= d)
        def _(d=d):
            for m in range(kv_count):
                dk, dv = second_pass(d, m)
                dkv[d - 1, 0, m] = dk.astype(bf16)
                dkv[d - 1, 1, m] = dv.astype(bf16)

            for w in (1, 0):
                @pl.when((d <= s) | (d == down))
                def _(w=w):
                    grad_home(d, w).start()

                @pl.when((d > s) & (d != down))
                def _(w=w):
                    grad_mate(d, w).start()

    @pl.when(z > 0)
    def _():
        for m in range(kv_count):
            dk, dv = second_pass(reach, m)
            sum4[0, m] = dk
            sum4[1, m] = dv

    for m in range(kv_count):
        dk, dv = second_pass(0, m)
        own_grad[0, m] = dk
        own_grad[1, m] = dv

    def rs_copy(w, j):
        return to_tp(part.at[w, j], rs_in.at[w, j - 1], rs_send.at[w, j - 1],
                     rs_recv.at[w, j - 1], lax.rem(t + j, n_tp))

    def project(w, lhs, index, by_row):
        block = lhs[index * local : (index + 1) * local, :]

        def step(i, carry):
            cols = pl.ds(pl.multiple_of(i * tile, 128), tile)
            if by_row:
                part[w, index, :, cols] = dot(block, wo[:, cols], 1, 0).astype(bf16)
            else:
                part[w, index, :, cols] = dot(block, wqkv[cols, :], 1, 1).astype(bf16)
            return carry

        lax.fori_loop(0, width // tile, step, 0)

    for j in range(1, n_tp):
        project(0, att, j, True)
        rs_copy(0, j).start()

    @pl.when(z > 0)
    def _():
        for w in (1, 0):
            span = spans[w]
            for k in range(1, reach):
                @pl.when(relays(k))
                def _(k=k, w=w, span=span):
                    to_ctx(zbuf.at[:, :, span], rin.at[k - 1, :, :, span], b_send.at[k - 1, w],
                           r_recv.at[k - 1, w], c).wait_recv()
                    sum4[:, :, span] += rin[k - 1, :, :, span].astype(f32)
            zbuf[:, :, span] = sum4[:, :, span].astype(bf16)
            grad_back(w).start()

    for m in range(kv_count):
        for g in range(per_kv):
            h = m * per_kv + g
            grad = dqt_s[m, :, g * rows : (g + 1) * rows].T
            u = raw[:, h * head : (h + 1) * head]
            back[:, h * head : (h + 1) * head] = norm_rope_back(
                grad, u, qgain[...], cos_t[...], sin_t[...], half
            ).astype(bf16)

    project(0, att, 0, True)

    def finish(w, base, dst):
        total = part[w, 0].astype(f32)
        for j in range(1, n_tp):
            rs_copy(w, j).wait_recv()
            total += rs_in[w, j - 1].astype(f32)
        stage[w] = (base[0].astype(f32) + total).astype(bf16)
        copy = pltpu.make_async_copy(stage.at[w], dst, out_sem.at[w])
        copy.start()
        return copy

    written = [finish(0, xg, out_ref)]

    def gin_add(d, w):
        span = spans[w]
        to_ctx(zbuf.at[:, :, span], gin.at[d - 1, :, :, span], b_send.at[d - 1, w],
               g_recv.at[d - 1, w], c).wait_recv()
        own_grad[:, :, span] += gin[d - 1, :, :, span].astype(f32)

    for w in (1, 0):
        span = spans[w]
        for d in range(1, reach):
            @pl.when(sends_own(d))
            def _(d=d, w=w):
                gin_add(d, w)

        @pl.when(z + 1 < nz)
        def _(w=w):
            gin_add(reach, w)

        for m in range(kv_count):
            k0 = qc + m * head
            u = raw[span, k0 : k0 + head]
            back[span, k0 : k0 + head] = norm_rope_back(
                own_grad[0, m, span], u, kgain[...], cos_t[span, :], sin_t[span, :], half
            ).astype(bf16)
            back[span, k0 + kc : k0 + kc + head] = own_grad[1, m, span].astype(bf16)

        if w == 0:
            project(1, back, 0, False)
        else:
            for j in range(1, n_tp):
                project(1, back, j, False)
                rs_copy(1, j).start()
    written.append(finish(1, gg, gout_ref))

    for w, copy in gathers:
        copy.wait_send()

    for w in range(2):
        @pl.when(z + 1 < nz)
        def _(w=w):
            ahead(w).wait_send()

        for k in range(1, reach):
            @pl.when(sends_own(k))
            def _(k=k, w=w):
                own_to(k, w).wait_send()

            @pl.when((z > 0) & relays(k))
            def _(k=k, w=w):
                relay_to(k, w).wait_send()

            @pl.when(c >= k)
            def _(k=k, w=w):
                grad_home(k, w).wait_send()

        @pl.when(z > 0)
        def _(w=w):
            grad_back(w).wait_send()

    for w in range(2):
        for j in range(1, n_tp):
            rs_copy(w, j).wait_send()
    for copy in written:
        copy.wait()


def on_device(
    tokens, result_grad, query_weight, key_weight, value_weight, output_weight, query_gain, key_gain
):
    n_ctx = lax.axis_size("ctx")
    n_tp = lax.axis_size("tp")
    local, width = tokens.shape
    rows = local * n_tp
    head = query_gain.shape[0]
    kv_count = key_weight.shape[1] // head
    per_kv = query_weight.shape[1] // key_weight.shape[1]
    reach = WINDOW // rows
    qc = kv_count * per_kv * head
    kc = kv_count * head
    qn = per_kv * rows
    tile = max(k for k in range(128, 1025, 128) if width % k == 0)
    exponent = np.arange(head // 2, dtype=np.float32) * np.float32(2.0 / head)
    frequency = np.power(np.float32(rope_theta), -exponent)
    frequency = jnp.asarray(np.concatenate([frequency, frequency])[None, :])
    any_spec = pl.BlockSpec(memory_space=pl.ANY)
    vmem_spec = pl.BlockSpec(memory_space=pltpu.VMEM)
    block = (2, kv_count, rows, head)
    dma = pltpu.SemaphoreType.DMA
    out = jax.ShapeDtypeStruct((local, width), bf16)
    return pl.pallas_call(
        functools.partial(kernel, n_ctx, n_tp, reach, per_kv, kv_count, head, tile),
        out_shape=(out, out),
        in_specs=[any_spec] * 6 + [vmem_spec] * 3,
        out_specs=(any_spec, any_spec),
        scratch_shapes=[
            pltpu.VMEM((width, qc + 2 * kc), bf16),
            pltpu.VMEM((qc, width), bf16),
            pltpu.VMEM((n_tp, local, width), bf16),
            pltpu.VMEM((n_tp, local, width), bf16),
            pltpu.VMEM((rows, qc + 2 * kc), f32),
            pltpu.VMEM((rows, head), f32),
            pltpu.VMEM((rows, head), f32),
            pltpu.VMEM((kv_count, qn, head), bf16),
            pltpu.VMEM((kv_count, qn, head), bf16),
            pltpu.VMEM((kv_count, head, qn), f32),
            pltpu.VMEM(block, bf16),
            pltpu.VMEM((reach,) + block, bf16),
            pltpu.VMEM((reach + 1, kv_count, rows, qn), bf16),
            pltpu.VMEM((reach + 1, kv_count, rows, qn), f32),
            pltpu.VMEM((kv_count, 1, qn), f32),
            pltpu.VMEM((kv_count, head, qn), f32),
            pltpu.VMEM((kv_count, head, qn), f32),
            pltpu.VMEM((rows, qc), bf16),
            pltpu.VMEM((reach - 1,) + block, bf16),
            pltpu.VMEM(block, f32),
            pltpu.VMEM(block, f32),
            pltpu.VMEM((reach,) + block, bf16),
            pltpu.VMEM((reach - 1,) + block, bf16),
            pltpu.VMEM(block, bf16),
            pltpu.VMEM((rows, qc + 2 * kc), bf16),
            pltpu.VMEM((2, n_tp, local, width), bf16),
            pltpu.VMEM((2, n_tp - 1, local, width), bf16),
            pltpu.VMEM((2, local, width), bf16),
            dma((6,)),
            dma((2, n_tp - 1)),
            dma((2, n_tp - 1)),
            dma((reach, 2)),
            dma((reach - 1, 2)),
            dma((reach, 2)),
            dma((reach, 2)),
            dma((reach, 2)),
            dma((reach - 1, 2)),
            dma((2, n_tp - 1)),
            dma((2, n_tp - 1)),
            dma((2,)),
        ],
        compiler_params=pltpu.CompilerParams(
            collective_id=0, has_side_effects=True, vmem_limit_bytes=60 * 1024 * 1024
        ),
    )(
        tokens, result_grad, query_weight, key_weight, value_weight, output_weight,
        query_gain[None, :], key_gain[None, :], frequency,
    )


def solution(mesh):
    in_specs = (
        P(("ctx", "tp"), None),
        P(("ctx", "tp"), None),
        P(None, "tp"),
        P(None, "tp"),
        P(None, "tp"),
        P("tp", None),
        P(),
        P(),
    )
    out_specs = (P(("ctx", "tp"), None), P(("ctx", "tp"), None))
    return jax.shard_map(
        on_device, mesh=mesh, in_specs=in_specs, out_specs=out_specs, check_vma=False
    )
```

profile of v0, /device:TPU:13, one launch (start us, length us, event | category | flops | bytes accessed | tf_op | source)
XLA Modules:
  0.0 34.9 jit_solution(9378714173469407244)
XLA Ops:
  0.6 31.3 %shard_map.104 = (bf16[128,2688]{1,0:T(8,128)(2,1)}, bf16[128,2688]{1,0:T(8,128)(2,1)}) custom-call(bf16[128,2688]{1,0:T(8,128)(2,1)} %tokens.1, bf16[128,2688]{1,0:T(8,128)(2,1)} %rgrad.1, bf16[2688,256]{1,0:T(8,128)(2,1)} %qw.1, bf16[2688,128]{1,0:T(8,128)(2,1)} %kw.1, bf16[2688,128]{1,0:T(8,128)(2,1)} %vw.1, bf16[256,2688]{1,0:T(8,128)(2,1)} %ow.1, ...), custom_call_target="tpu_custom_call" | custom-call | tf_op jit(solution)/shard_map/pallas_call | solution.py:477
  32.0 0.0 copy-start
  32.0 2.1 %copy.13 = bf16[128,2688]{1,0:T(8,128)(2,1)} copy(bf16[128,2688]{1,0:T(8,128)(2,1)} %get-tuple-element.4) | data formatting | bytes 1376256
  34.0 0.0 copy-done
  34.0 0.8 %copy.14 = bf16[128,2688]{1,0:T(8,128)(2,1)} copy(bf16[128,2688]{1,0:T(8,128)(2,1)S(1)} %copy-done) | data formatting | bytes 1376256
Async XLA Ops:
  32.0 2.1 %copy-start = (bf16[128,2688]{1,0:T(8,128)(2,1)S(1)}, bf16[128,2688]{1,0:T(8,128)(2,1)}, u32[]{:S(2)}) copy-start(bf16[128,2688]{1,0:T(8,128)(2,1)} %get-tuple-element.5) | copy-start | bytes 2064388
where the time goes:
time: 35 us; the launch traced here: 34.9 us
  Pallas kernels  31.3 us (89%)
  local copies, waits for them, and re-layouts  2.91 us (8%)
  between operations  0.65 us (2%)
    pallas_call x1, Pallas kernels, on_device(): pl.pallas_call(functools.partial(kernel, n_ctx, n_tp, reach, per_kv, kv_c...  31.3 us
    unnamed x4, local copies, waits for them, and re-layouts  2.91 us

commit v1 on v0

v1 whole, which is shorter than its diff:
```python
import functools

import jax
import jax.numpy as jnp
import numpy as np
from jax import lax
from jax.experimental import pallas as pl
from jax.experimental.pallas import tpu as pltpu
from jax.sharding import PartitionSpec as P

WINDOW = 1024
norm_epsilon = 1e-06
score_scale = 168.0 ** (-0.5)
rope_theta = 10000.0
MESH = pl.DeviceIdType.MESH
TREE = (
    (0, 1, 0, (0, 1)), (0, 2, 0, (0, 1)), (1, 3, 0, (0, 1)), (2, 3, 0, (0, 1)),
    (1, 0, 4, (0, 1)), (2, 0, 4, (0, 1)), (3, 2, 4, (0, 1)), (3, 1, 4, (0, 1)),
    (1, 3, 1, (0,)), (2, 3, 2, (1,)), (3, 2, 2, (0, 1)),
    (1, 0, 2, (0,)), (2, 0, 3, (1,)), (0, 1, 2, (0, 1)),
)
f32 = jnp.float32
bf16 = jnp.bfloat16


def dot(a, b, ca, cb):
    return lax.dot_general(a, b, (((ca,), (cb,)), ((), ())), preferred_element_type=f32)


def rope(n, cosines, sines, half):
    return n * cosines + pltpu.roll(n, half, 1) * sines


def rope_back(g, cosines, sines, half):
    return g * cosines + pltpu.roll(g * sines, half, 1)


def inverse_rms(u):
    return lax.rsqrt(jnp.mean(u * u, axis=-1, keepdims=True) + norm_epsilon)


def norm_rope_back(g, u, gain, cosines, sines, half):
    r = inverse_rms(u)
    w = rope_back(g, cosines, sines, half) * gain
    return r * (w - u * (r * r * jnp.mean(w * u, axis=-1, keepdims=True)))


def axis_of(a, b):
    return 0 if a ^ b == 1 else 1


def children(place, d, w):
    return [(b, d + b - a, axis_of(a, b)) for a, b, e, ws in TREE if (a, e) == (place, d) and w in ws]


def parent(place, d, w):
    (a,) = [(a, e, axis_of(a, b)) for a, b, e, ws in TREE if (b, e + b - a) == (place, d) and w in ws]
    return a


def slot(place, d, axis, w):
    if axis == 2:
        return w
    seen = [(e, axis_of(a, b), v) for a, b, e, ws in TREE if a == place for v in ws]
    return 2 + seen.index((d, axis, w))


SLOTS = 2 + max(sum(len(ws) for a, _, _, ws in TREE if a == place) for place in range(4))


def kernel(
    n_ctx, n_tp, reach, per_kv, kv_count, head, tiles,
    tokens, rgrad, qw, kw, vw, ow, qgain_in, kgain_in, freq_in,
    out_ref, gout_ref,
    wqkv, wo, xg, gg, raw, cos_t, sin_t, q_s, do_s, dot_s, kv_own, halo, e_s, dp_s,
    l_s, ot_s, dqt_s, att, dkv, own_grad, gin, back, part, rs_in, acc, rope_in,
    local_sem, ag_send, ag_recv, f_send, f_recv, b_send, b_recv, rs_send, rs_recv,
):
    c = lax.axis_index("ctx")
    t = lax.axis_index("tp")
    s = lax.rem(c, reach)
    z = lax.div(c, reach)
    nz = n_ctx // reach
    local, width = xg.shape[1], xg.shape[2]
    rows = local * n_tp
    half = head // 2
    qc = kv_count * per_kv * head
    kc = kv_count * head
    qn = per_kv * rows

    barrier = pltpu.get_barrier_semaphore()
    for j in range(1, n_tp):
        pl.semaphore_signal(
            barrier, inc=1, device_id={"tp": lax.rem(t + j, n_tp)}, device_id_type=MESH
        )
    mates = (c + 1 - 2 * lax.rem(s, 2), c + 2 - 4 * lax.div(s, 2))
    for mate in mates:
        pl.semaphore_signal(barrier, inc=1, device_id={"ctx": mate}, device_id_type=MESH)

    @pl.when(z + 1 < nz)
    def _():
        pl.semaphore_signal(barrier, inc=1, device_id={"ctx": c + reach}, device_id_type=MESH)

    @pl.when(z > 0)
    def _():
        pl.semaphore_signal(barrier, inc=1, device_id={"ctx": c - reach}, device_id_type=MESH)

    def local_copy(i, src, dst):
        return pltpu.make_async_copy(src, dst, local_sem.at[i])

    loads = [
        local_copy(0, tokens, xg.at[0]),
        local_copy(1, qw, wqkv.at[:, :qc]),
        local_copy(2, rgrad, gg.at[0]),
        local_copy(3, ow, wo),
    ]
    kv_loads = [
        local_copy(4, kw, wqkv.at[:, qc : qc + kc]),
        local_copy(4, vw, wqkv.at[:, qc + kc : qc + 2 * kc]),
    ]
    table_loads = [local_copy(5, x, rope_in.at[i]) for i, x in enumerate((freq_in, kgain_in, qgain_in))]
    for load in table_loads + loads[:1] + kv_loads + loads[1:]:
        load.start()

    def to_ctx(src, dst, send, recv, target):
        return pltpu.make_async_remote_copy(
            src_ref=src, dst_ref=dst, send_sem=send, recv_sem=recv,
            device_id={"ctx": target}, device_id_type=MESH,
        )

    def to_tp(src, dst, send, recv, target):
        return pltpu.make_async_remote_copy(
            src_ref=src, dst_ref=dst, send_sem=send, recv_sem=recv,
            device_id={"tp": target}, device_id_type=MESH,
        )

    one, none = jnp.int32(1), jnp.int32(0)
    greeted = n_tp - 1 + 2 + jnp.where(z > 0, one, none) + jnp.where(z + 1 < nz, one, none)
    pl.semaphore_wait(barrier, greeted)

    def gather(w, j):
        src, dst = (tokens, xg) if w == 0 else (rgrad, gg)
        return to_tp(src, dst.at[n_tp - j], ag_send, ag_recv.at[w, j - 1],
                     lax.rem(t + j, n_tp))

    for j in range(1, n_tp):
        gather(0, j).start()

    def place(row):
        return lax.rem(t + lax.div(row, local), n_tp) * local + lax.rem(row, local)

    local_copy(5, rope_in, rope_in).wait()
    freq, kgain, qgain = rope_in.at[0], rope_in.at[1], rope_in.at[2]
    fold = rows // 2
    lane = lax.broadcasted_iota(jnp.int32, (fold, head), 1)
    low_lanes = lane < half
    row = lax.broadcasted_iota(jnp.int32, (fold, head), 0) + jnp.where(low_lanes, 0, fold)
    angles = (c * rows + place(row)).astype(f32) * freq[...]
    cosines, sines = jnp.cos(angles), jnp.sin(angles)
    cos_r, sin_r = pltpu.roll(cosines, half, 1), pltpu.roll(sines, half, 1)
    cos_t[:fold, :] = jnp.where(low_lanes, cosines, cos_r)
    cos_t[fold:, :] = jnp.where(low_lanes, cos_r, cosines)
    sin_t[:fold, :] = jnp.where(low_lanes, -sines, sin_r)
    sin_t[fold:, :] = jnp.where(low_lanes, -sin_r, sines)

    spans = (slice(0, local), slice(local, rows))
    chunks = [(w, i) for w in range(2) for i in range(2)]

    def key_values(w, x):
        span = spans[w]
        raw[span, qc : qc + 2 * kc] = dot(x, wqkv[:, qc : qc + 2 * kc], 1, 0)
        for m in range(kv_count):
            u = raw[span, qc + m * head : qc + (m + 1) * head]
            n = u * inverse_rms(u) * kgain[...]
            kv_own[0, m, span] = rope(n, cos_t[span, :], sin_t[span, :], half).astype(bf16)
            v0 = qc + kc + m * head
            kv_own[1, m, span] = raw[span, v0 : v0 + head].astype(bf16)

    def hop(a, b, d, w, i):
        span, e = spans[w], d + b - a
        src = kv_own.at[i, :, span] if d == 0 else halo.at[d - 1, i, :, span]
        return to_ctx(src, halo.at[e - 1, i, :, span], f_send.at[int(d > a)],
                      f_recv.at[e - 1, w, i], c + b - a)

    def ahead(w, i):
        span = spans[w]
        return to_ctx(kv_own.at[i, :, span], halo.at[reach - 1, i, :, span],
                      f_send.at[2], f_recv.at[reach - 1, w, i], c + reach)

    def arrived(d, w, i):
        span = spans[w]
        to_ctx(kv_own.at[i, :, span], halo.at[d - 1, i, :, span], f_send.at[2],
               f_recv.at[d - 1, w, i], c).wait_recv()

    def at(k, a, d):
        return (s == k) & (z > 0) if d > a else s == k

    def relay(jobs):
        for k in range(reach):
            for early in (True, False):
                mine = [j for j in jobs if j[0] == k and (j[1] > k) == early]
                if mine:
                    @pl.when((s == k) & (z > 0) if early else s == k)
                    def _(mine=mine):
                        for a, d, w in mine:
                            for i in range(2):
                                arrived(d, w, i)
                                for b, ws in [(b, ws) for x, b, e, ws in TREE if (x, e) == (a, d)]:
                                    if w in ws:
                                        hop(a, b, d, w, i).start()

    for w in range(2):
        if w == 0:
            loads[0].wait()
            local_copy(4, wqkv.at[:, qc:], wqkv.at[:, qc:]).wait()
            key_values(w, xg[0])
        else:
            for j in range(1, n_tp):
                gather(0, j).wait_recv()
            key_values(w, xg[1:].reshape(rows - local, width))

        @pl.when(z + 1 < nz)
        def _(w=w):
            for i in range(2):
                ahead(w, i).start()

        for k in range(reach - 1):
            @pl.when(s == k)
            def _(k=k, w=w):
                for i in range(2):
                    for b, _, _ in children(k, 0, w):
                        hop(k, b, 0, w, i).start()

    for j in range(1, n_tp):
        gather(1, j).start()
    loads[1].wait()
    raw[:, :qc] = dot(xg[...].reshape(rows, width), wqkv[:, :qc], 1, 0)
    for h in range(kv_count * per_kv):
        m, g = h // per_kv, h % per_kv
        u = raw[:, h * head : (h + 1) * head]
        n = u * inverse_rms(u) * qgain[...]
        q_s[m, g * rows : (g + 1) * rows] = rope(n, cos_t[...], sin_t[...], half).astype(bf16)
    relay([(1, 4, 0), (2, 4, 0), (3, 4, 0), (1, 1, 0), (3, 2, 0)])

    loads[2].wait()
    loads[3].wait()
    for j in range(1, n_tp):
        gather(1, j).wait_recv()
    d_out = dot(gg[...].reshape(rows, width), wo[...], 1, 1).astype(bf16)
    for h in range(kv_count * per_kv):
        m, g = h // per_kv, h % per_kv
        piece = d_out[:, h * head : (h + 1) * head]
        do_s[m, g * rows : (g + 1) * rows] = piece
        dot_s[m, :, g * rows : (g + 1) * rows] = piece.astype(f32).T
    relay([(1, 4, 1), (2, 4, 1), (3, 4, 1), (2, 2, 1), (3, 2, 1)])

    def kv(d, w, m):
        return kv_own[w, m] if isinstance(d, int) and d == 0 else halo[d - 1, w, m]

    def first_pass(d):
        for m in range(kv_count):
            key, value = kv(d, 0, m), kv(d, 1, m)
            e = jnp.exp(dot(key, q_s[m], 1, 1) * score_scale)
            if isinstance(d, int):
                key_row = place(lax.broadcasted_iota(jnp.int32, (rows, 1), 0))
                query_row = place(
                    lax.rem(lax.broadcasted_iota(jnp.int32, (1, qn), 1), jnp.int32(rows))
                )
                keep = query_row >= key_row if d == 0 else query_row < key_row
                e = jnp.where(keep, e, f32(0.0))
            total = jnp.sum(e, axis=0, keepdims=True)
            low = e.astype(bf16)
            e_s[d, m] = low
            mixed = dot(value, low, 0, 0)
            dp_s[d, m] = dot(value, do_s[m], 1, 1) * score_scale
            if isinstance(d, int) and d == 0:
                l_s[m] = total
                ot_s[m] = mixed
            else:
                l_s[m] += total
                ot_s[m] += mixed

    first_pass(0)
    relay([(1, 2, 0), (0, 2, 0)])

    @pl.when(z > 0)
    def _():
        for k in (0,):
            @pl.when(s == k)
            def _():
                for w, i in chunks:
                    arrived(reach, w, i)
        first_pass(reach)

    relay([(2, 3, 1), (0, 2, 1)])

    def pick(*by_place):
        value = jnp.int32(by_place[0])
        for k in range(1, reach):
            value = jnp.where(s == k, jnp.int32(by_place[k]), value)
        return value

    relayed = {(1, 4, 0), (2, 4, 0), (3, 4, 0), (1, 1, 0), (3, 2, 0), (1, 4, 1), (2, 4, 1), (3, 4, 1),
               (2, 2, 1), (3, 2, 1), (1, 2, 0), (0, 2, 0), (2, 3, 1), (0, 2, 1)}
    order = ((3, 2, 1), (1, 2, 3), (2, 1, 3), (1, 2, 3))
    for step in range(reach - 1):
        for k in range(reach):
            d = order[k][step]

            @pl.when((s == k) & (z > 0) if d > k else s == k)
            def _(k=k, d=d):
                for w, i in chunks:
                    if (k, d, w) not in relayed:
                        arrived(d, w, i)

        far = pick(*[order[k][step] for k in range(reach)])

        @pl.when(c >= far)
        def _(far=far):
            first_pass(far)

    inv, delta = [], []
    for m in range(kv_count):
        inv.append(1.0 / l_s[m])
        o_t = (ot_s[m] * inv[m]).astype(bf16).astype(f32)
        delta.append(jnp.sum(o_t * dot_s[m], axis=0, keepdims=True) * score_scale)
        for g in range(per_kv):
            h = m * per_kv + g
            att[:, h * head : (h + 1) * head] = o_t[:, g * rows : (g + 1) * rows].T.astype(bf16)
        dqt_s[m] = jnp.zeros_like(dqt_s[m])

    def second_pass(d, m):
        p = e_s[d, m].astype(f32) * inv[m]
        ds = (p * (dp_s[d, m] - delta[m])).astype(bf16)
        dk = dot(ds, q_s[m], 1, 0)
        dv = dot(p.astype(bf16), do_s[m], 1, 0)
        dqt_s[m] += dot(kv(d, 0, m), ds, 0, 0)
        return dk, dv

    def give(k, d, w, i):
        span = spans[w]
        if d == reach:
            return to_ctx(dkv.at[d - 1, i, :, span], gin.at[0, 2, i, :, span],
                          b_send.at[1], b_recv.at[slot(k, 0, 2, w), i], c - reach)
        a, e, axis = parent(k, d, w)
        return to_ctx(dkv.at[d - 1, i, :, span], gin.at[e, axis, i, :, span],
                      b_send.at[int(d > k)], b_recv.at[slot(a, e, axis, w), i], c + a - k)

    def taken(k, d, axis, w, i):
        span = spans[w]
        to_ctx(dkv.at[0, i, :, span], gin.at[d, axis, i, :, span], b_send.at[0],
               b_recv.at[slot(k, d, axis, w), i], c).wait_recv()
        return gin[d, axis, i, :, span].astype(f32)

    def combine(jobs):
        for k in range(reach):
            for early in (True, False):
                mine = [j for j in jobs if j[0] == k and (j[1] > k) == early]
                if mine:
                    @pl.when((s == k) & (z > 0) if early else s == k)
                    def _(mine=mine):
                        for k, d, w in mine:
                            for i in range(2):
                                span = spans[w]
                                total = dkv[d - 1, i, :, span].astype(f32)
                                for _, _, axis in children(k, d, w):
                                    total += taken(k, d, axis, w, i)
                                dkv[d - 1, i, :, span] = total.astype(bf16)
                                give(k, d, w, i).start()

    for d in (1, 3, 2, 4):
        @pl.when(c >= d)
        def _(d=d):
            for m in range(kv_count):
                dk, dv = second_pass(d, m)
                dkv[d - 1, 0, m] = dk.astype(bf16)
                dkv[d - 1, 1, m] = dv.astype(bf16)
            for k in range(reach):
                leaves = [w for w in (1, 0) if not children(k, d, w)]
                if leaves:
                    @pl.when(s == k)
                    def _(k=k, leaves=leaves):
                        for w in leaves:
                            for i in range(2):
                                give(k, d, w, i).start()

    for m in range(kv_count):
        dk, dv = second_pass(0, m)
        own_grad[0, m] = dk
        own_grad[1, m] = dv

    def rs_copy(w, j, n):
        cols = slice(*tiles[n])
        return to_tp(part.at[w, j, :, cols], rs_in.at[w, j - 1, :, cols], rs_send,
                     rs_recv.at[w, j - 1, n], lax.rem(t + j, n_tp))

    def product(lhs, n, first, last, by_row):
        cols = slice(*tiles[n])
        if by_row:
            return dot(lhs, wo[:, cols], 1, 0)
        return dot(lhs, wqkv[cols, first:last], 1, 1)

    def project(w, lhs, base, first, last, by_row):
        for n, (lo, hi) in enumerate(tiles):
            both = product(lhs, n, first, last, by_row)
            acc[w, :, lo:hi] = base[0, :, lo:hi].astype(f32) + both[:local]
            for j in range(1, n_tp):
                part[w, j, :, lo:hi] = both[j * local : (j + 1) * local].astype(bf16)
                rs_copy(w, j, n).start()

    project(0, att[...], xg, 0, qc, True)
    for m in range(kv_count):
        for g in range(per_kv):
            h = m * per_kv + g
            grad = dqt_s[m, :, g * rows : (g + 1) * rows].T
            u = raw[:, h * head : (h + 1) * head]
            back[:, h * head : (h + 1) * head] = norm_rope_back(
                grad, u, qgain[...], cos_t[...], sin_t[...], half
            ).astype(bf16)
    combine([(0, 2, 1), (0, 2, 0), (2, 3, 1), (2, 2, 1), (3, 2, 1), (3, 2, 0),
             (1, 2, 0), (1, 4, 1), (1, 4, 0), (1, 1, 0)])
    project(1, back[:, :qc], gg, 0, qc, False)
    combine([(2, 4, 1), (2, 4, 0), (3, 4, 1), (3, 4, 0)])

    def landed(w, n):
        lo, hi = tiles[n]
        total = acc[w if w < 2 else 1, :, lo:hi]
        for j in range(1, n_tp):
            rs_copy(w, j, n).wait_recv()
            total += rs_in[w, j - 1, :, lo:hi].astype(f32)
        return total

    for n, (lo, hi) in enumerate(tiles):
        out_ref[:, lo:hi] = landed(0, n).astype(bf16)
    for n, (lo, hi) in enumerate(tiles):
        acc[1, :, lo:hi] = landed(1, n)

    for w in (1, 0):
        span = spans[w]
        for i in range(2):
            for k in range(reach):
                kids = children(k, 0, w)
                if kids:
                    @pl.when(s == k)
                    def _(kids=kids, w=w, i=i, span=span, k=k):
                        for _, _, axis in kids:
                            own_grad[i, :, span] += taken(k, 0, axis, w, i)

            @pl.when(z + 1 < nz)
            def _(w=w, i=i, span=span):
                own_grad[i, :, span] += taken(0, 0, 2, w, i)

        for m in range(kv_count):
            k0 = qc + m * head
            u = raw[span, k0 : k0 + head]
            back[span, k0 : k0 + head] = norm_rope_back(
                own_grad[0, m, span], u, kgain[...], cos_t[span, :], sin_t[span, :], half
            ).astype(bf16)
            back[span, k0 + kc : k0 + kc + head] = own_grad[1, m, span].astype(bf16)

        for n, (lo, hi) in enumerate(tiles):
            piece = product(back[span, qc:], n, qc, qc + 2 * kc, False)
            if w == 0:
                acc[1, :, lo:hi] += piece
            else:
                for j in range(1, n_tp):
                    part[2, j, :, lo:hi] = piece[(j - 1) * local : j * local].astype(bf16)
                    rs_copy(2, j, n).start()
    for n, (lo, hi) in enumerate(tiles):
        gout_ref[:, lo:hi] = landed(2, n).astype(bf16)

    def sent(sem, ref):
        pltpu.make_async_copy(ref, ref, sem).wait()

    sent(ag_send, part.at[:2, 1:])
    sent(rs_send, part.at[:, 1:])

    @pl.when(z + 1 < nz)
    def _():
        sent(f_send.at[2], kv_own)

    for k in range(reach):
        for early in (True, False):
            @pl.when((s == k) & (z > 0) if early else s == k)
            def _(k=k, early=early):
                halves = sum(len(ws) for a, b, d, ws in TREE if a == k and (d > k) == early)
                if halves // 2:
                    sent(f_send.at[int(early)], halo.at[: halves // 2])
                if halves % 2:
                    sent(f_send.at[int(early)], halo.at[0, :, :, spans[0]])
                first, last = (k, reach) if early else (0, k)
                if first < last:
                    sent(b_send.at[int(early)], dkv.at[first:last])


def write(a, b, a_out, b_out, sems):
    split = sems.shape[1]
    step = a.shape[0] // split
    copies = [
        pltpu.make_async_copy(x.at[pl.ds(i * step, step)], y.at[pl.ds(i * step, step)], sems.at[w, i])
        for w, (x, y) in enumerate(((a, a_out), (b, b_out)))
        for i in range(split)
    ]
    for copy in copies:
        copy.start()
    for copy in copies:
        copy.wait()


def on_device(
    tokens, result_grad, query_weight, key_weight, value_weight, output_weight, query_gain, key_gain
):
    n_ctx = lax.axis_size("ctx")
    n_tp = lax.axis_size("tp")
    local, width = tokens.shape
    rows = local * n_tp
    head = query_gain.shape[0]
    kv_count = key_weight.shape[1] // head
    per_kv = query_weight.shape[1] // key_weight.shape[1]
    reach = WINDOW // rows
    assert reach == 4 and n_ctx % reach == 0
    qc = kv_count * per_kv * head
    kc = kv_count * head
    qn = per_kv * rows
    tiles = tuple((lo, min(lo + 1024, width)) for lo in range(0, width, 1024))
    exponent = np.arange(head // 2, dtype=np.float32) * np.float32(2.0 / head)
    frequency = np.power(np.float32(rope_theta), -exponent)
    frequency = jnp.asarray(np.concatenate([frequency, frequency])[None, :])
    any_spec = pl.BlockSpec(memory_space=pl.ANY)
    vmem_spec = pl.BlockSpec(memory_space=pltpu.VMEM)
    block = (2, kv_count, rows, head)
    dma = pltpu.SemaphoreType.DMA
    out = pltpu.VMEM((local, width), bf16)
    layer_output, tokens_grad = pl.pallas_call(
        functools.partial(kernel, n_ctx, n_tp, reach, per_kv, kv_count, head, tiles),
        out_shape=(out, out),
        in_specs=[any_spec] * 9,
        out_specs=(vmem_spec, vmem_spec),
        scratch_shapes=[
            pltpu.VMEM((width, qc + 2 * kc), bf16),
            pltpu.VMEM((qc, width), bf16),
            pltpu.VMEM((n_tp, local, width), bf16),
            pltpu.VMEM((n_tp, local, width), bf16),
            pltpu.VMEM((rows, qc + 2 * kc), f32),
            pltpu.VMEM((rows, head), f32),
            pltpu.VMEM((rows, head), f32),
            pltpu.VMEM((kv_count, qn, head), bf16),
            pltpu.VMEM((kv_count, qn, head), bf16),
            pltpu.VMEM((kv_count, head, qn), f32),
            pltpu.VMEM(block, bf16),
            pltpu.VMEM((reach,) + block, bf16),
            pltpu.VMEM((reach + 1, kv_count, rows, qn), bf16),
            pltpu.VMEM((reach + 1, kv_count, rows, qn), f32),
            pltpu.VMEM((kv_count, 1, qn), f32),
            pltpu.VMEM((kv_count, head, qn), f32),
            pltpu.VMEM((kv_count, head, qn), f32),
            pltpu.VMEM((rows, qc), bf16),
            pltpu.VMEM((reach,) + block, bf16),
            pltpu.VMEM(block, f32),
            pltpu.VMEM((reach + 1, 3) + block, bf16),
            pltpu.VMEM((rows, qc + 2 * kc), bf16),
            pltpu.VMEM((3, n_tp, local, width), bf16),
            pltpu.VMEM((3, n_tp - 1, local, width), bf16),
            pltpu.VMEM((2, local, width), f32),
            pltpu.VMEM((3, 1, head), f32),
            dma((6,)),
            dma,
            dma((2, n_tp - 1)),
            dma((3,)),
            dma((reach, 2, 2)),
            dma((2,)),
            dma((SLOTS, 2)),
            dma,
            dma((3, n_tp - 1, len(tiles))),
        ],
        compiler_params=pltpu.CompilerParams(
            collective_id=0, has_side_effects=True, vmem_limit_bytes=56 * 1024 * 1024
        ),
    )(
        tokens, result_grad, query_weight, key_weight, value_weight, output_weight,
        query_gain[None, :], key_gain[None, :], frequency,
    )
    result = jax.ShapeDtypeStruct((local, width), bf16)
    return pl.pallas_call(
        write,
        out_shape=(result, result),
        in_specs=[vmem_spec] * 2,
        out_specs=(any_spec, any_spec),
        scratch_shapes=[dma((2, 4 if local % 64 == 0 else 1))],
        compiler_params=pltpu.CompilerParams(vmem_limit_bytes=2 * 1024 * 1024),
    )(layer_output, tokens_grad)


def solution(mesh):
    in_specs = (
        P(("ctx", "tp"), None),
        P(("ctx", "tp"), None),
        P(None, "tp"),
        P(None, "tp"),
        P(None, "tp"),
        P("tp", None),
        P(),
        P(),
    )
    out_specs = (P(("ctx", "tp"), None), P(("ctx", "tp"), None))
    return jax.shard_map(
        on_device, mesh=mesh, in_specs=in_specs, out_specs=out_specs, check_vma=False
    )
```

time: 35 us -> 31.1 us (0.89)
  the two profiles are of different devices: /device:TPU:13 before, /device:TPU:15 now
where the time goes in v1:
time: 31.1 us; the launch traced here: 30.9 us
  Pallas kernels  30.3 us (97%)
  between operations  0.64 us (2%)
    pallas_call x1, Pallas kernels, on_device(): pl.pallas_call(functools.partial(kernel, n_ctx, n_tp, reach, per_kv, kv_c...  29.1 us
    pallas_call x1, Pallas kernels, on_device(): pl.pallas_call(write, out_shape=(result, result), in_specs=[vmem_spec] *...  1.14 us

profile of v1, /device:TPU:15, one launch (start us, length us, event | category | flops | bytes accessed | tf_op | source)
XLA Modules:
  0.0 30.9 jit_solution(13801093685913147305)
XLA Ops:
  0.6 29.1 %shard_map.104 = (bf16[128,2688]{1,0:T(8,128)(2,1)S(1)}, bf16[128,2688]{1,0:T(8,128)(2,1)S(1)}) custom-call(bf16[128,2688]{1,0:T(8,128)(2,1)} %tokens.1, bf16[128,2688]{1,0:T(8,128)(2,1)} %rgrad.1, bf16[2688,256]{1,0:T(8,128)(2,1)} %qw.1, bf16[2688,128]{1,0:T(8,128)(2,1)} %kw.1, bf16[2688,128]{1,0:T(8,128)(2,1)} %vw.1, bf16[256,2688]{1,0:T(8,128)(2,1)} %ow.1, ...), custom_call_target="tpu_custom_call" | custom-call | tf_op jit(solution)/shard_map/pallas_call | solution.py:534
  29.8 1.1 %shard_map.105 = (bf16[128,2688]{1,0:T(8,128)(2,1)}, bf16[128,2688]{1,0:T(8,128)(2,1)}) custom-call(bf16[128,2688]{1,0:T(8,128)(2,1)S(1)} %get-tuple-element.4.a, bf16[128,2688]{1,0:T(8,128)(2,1)S(1)} %get-tuple-element.5.b), custom_call_target="tpu_custom_call" | custom-call | tf_op jit(solution)/shard_map/pallas_call | solution.py:584

commit v2 on v1

--- a/solution.py
+++ b/solution.py
@@ -19,6 +19,33 @@
     (1, 3, 1, (0,)), (2, 3, 2, (1,)), (3, 2, 2, (0, 1)),
     (1, 0, 2, (0,)), (2, 0, 3, (1,)), (0, 1, 2, (0, 1)),
 )
+OUT = (
+    (0, 0, 1, 0, 0), (1, 3, 0, 0, 0), (2, 3, 0, 0, 0), (1, 1, 1, 0, 0), (0, 2, 0, 0, 0),
+    (3, 2, 1, 0, 0), (1, 2, 0, 0, 0), (1, 0, 1, 0, 0), (0, 1, 0, 0, 0), (2, 0, 1, 0, 0),
+    (0, 2, 0, 0, 1), (0, 1, 0, 0, 1), (2, 3, 0, 0, 1), (1, 0, 1, 0, 1), (0, 0, 1, 0, 1),
+    (3, 1, 1, 0, 1), (1, 1, 1, 0, 1), (2, 0, 1, 0, 1), (2, 2, 1, 0, 1), (1, 3, 0, 0, 1),
+    (3, 2, 1, 0, 1), (3, 3, 1, 0, 1), (1, 3, 0, 1, 0), (2, 0, 0, 3, 0), (2, 1, 0, 3, 0),
+    (0, 1, 0, 2, 0), (0, 2, 0, 2, 0), (2, 3, 0, 3, 0), (1, 3, 0, 1, 1), (3, 2, 0, 2, 1),
+    (0, 1, 0, 2, 1), (1, 0, 0, 2, 1),
+)
+HOME = (
+    (1, 0, 0, 3, 1), (3, 3, -1, 4, 0), (3, 0, 0, 3, 0), (1, 1, -1, 4, 0), (0, 2, 0, 1, 1),
+    (3, 2, 0, 1, 1), (0, 0, -1, 4, 1), (0, 1, 0, 3, 1), (2, 3, -1, 3, 1), (2, 1, 0, 1, 1),
+    (1, 0, 0, 1, 0), (2, 3, 0, 1, 0), (3, 1, 0, 2, 0), (0, 0, -1, 4, 0), (1, 0, 0, 1, 1),
+    (3, 1, 0, 2, 1), (2, 2, -1, 4, 0), (0, 1, 0, 3, 0), (3, 2, 0, 1, 0), (1, 1, -1, 4, 1),
+    (3, 2, 0, 4, 1), (0, 2, -1, 2, 0), (0, 2, 0, 1, 0), (0, 2, -1, 2, 1), (1, 0, 0, 3, 0),
+    (2, 3, -1, 3, 0), (1, 3, -1, 2, 1), (2, 0, 0, 2, 0), (1, 3, -1, 2, 0), (2, 2, -1, 4, 1),
+    (3, 1, 0, 3, 1), (2, 0, 0, 2, 1),
+)
+PASS_ON = (
+    (), ((1, 1, 0), (0, 2, 0), (2, 3, 0)), ((1, 1, 1), (3, 2, 1)), ((0, 2, 1), (1, 2, 1)), (),
+)
+ADD_UP = (
+    (), (), ((0, 2, 1), (2, 3, 1)), ((1, 4, 1), (0, 2, 0)), ((1, 1, 1), (2, 3, 0), (3, 2, 0), (1, 4, 0)),
+)
+FIRST = ((4, 2, 3, 1), (1, 2, 4, 3), (2, 3, 4, 1), (2, 1, 4, 3))
+SECOND = ((4, 1, 3, 2), (3, 2, 1, 4), (4, 1, 2, 3), (4, 3, 1, 2))
+GROUP = 4
 f32 = jnp.float32
 bf16 = jnp.bfloat16
 
@@ -66,6 +93,39 @@
 
 
 SLOTS = 2 + max(sum(len(ws) for a, _, _, ws in TREE if a == place) for place in range(4))
+
+
+def step_of(a, b, ahead):
+    return GROUP * ahead + b - a
+
+
+def out_of(place, d, w):
+    return [(b, g) for a, b, g, e, v in OUT if (a, e, v) == (place, d, w)]
+
+
+def home_of(place, d, w):
+    ((b, g),) = [(b, g) for a, b, g, e, v in HOME if (a, e, v) == (place, d, w)]
+    return b, g
+
+
+def inbound(place):
+    return [(a, e, g, v) for a, b, g, e, v in HOME if b == place]
+
+
+def givers(place, d, w):
+    return [
+        (a, e, g) for a, e, g, v in inbound(place)
+        if v == w and e + step_of(a, place, g) == d
+    ]
+
+
+def partners(place, g):
+    pairs = {(a, b, h) for a, b, h, _, _ in OUT + HOME}
+    pairs |= {(b, a, -h) for a, b, h in pairs}
+    return sorted(b for a, b, h in pairs if (a, h) == (place, g) and (b, g) != (place, 0))
+
+
+SLOTS = max(len(inbound(place)) for place in range(GROUP))
 
 
 def kernel(
@@ -93,17 +153,30 @@
         pl.semaphore_signal(
             barrier, inc=1, device_id={"tp": lax.rem(t + j, n_tp)}, device_id_type=MESH
         )
-    mates = (c + 1 - 2 * lax.rem(s, 2), c + 2 - 4 * lax.div(s, 2))
-    for mate in mates:
-        pl.semaphore_signal(barrier, inc=1, device_id={"ctx": mate}, device_id_type=MESH)
-
-    @pl.when(z + 1 < nz)
-    def _():
-        pl.semaphore_signal(barrier, inc=1, device_id={"ctx": c + reach}, device_id_type=MESH)
-
-    @pl.when(z > 0)
-    def _():
-        pl.semaphore_signal(barrier, inc=1, device_id={"ctx": c - reach}, device_id_type=MESH)
+    def here(k, early=False, later=False):
+        on = s == k
+        if early:
+            on = on & (z > 0)
+        if later:
+            on = on & (z + 1 < nz)
+        return on
+
+    def pick(by_place):
+        value = jnp.int32(by_place[0])
+        for k in range(1, reach):
+            value = jnp.where(s == k, jnp.int32(by_place[k]), value)
+        return value
+
+    for k in range(reach):
+        for g in (-1, 0, 1):
+            if partners(k, g):
+                @pl.when(here(k, early=g < 0, later=g > 0))
+                def _(k=k, g=g):
+                    for b in partners(k, g):
+                        pl.semaphore_signal(
+                            barrier, inc=1, device_id={"ctx": c + step_of(k, b, g)},
+                            device_id_type=MESH,
+                        )
 
     def local_copy(i, src, dst):
         return pltpu.make_async_copy(src, dst, local_sem.at[i])
@@ -134,18 +207,14 @@
             device_id={"tp": target}, device_id_type=MESH,
         )
 
-    one, none = jnp.int32(1), jnp.int32(0)
-    greeted = n_tp - 1 + 2 + jnp.where(z > 0, one, none) + jnp.where(z + 1 < nz, one, none)
-    pl.semaphore_wait(barrier, greeted)
-
-    def gather(w, j):
-        src, dst = (tokens, xg) if w == 0 else (rgrad, gg)
-        return to_tp(src, dst.at[n_tp - j], ag_send, ag_recv.at[w, j - 1],
-                     lax.rem(t + j, n_tp))
-
-    for j in range(1, n_tp):
-        gather(0, j).start()
-
+    count = [[len(partners(k, g)) for k in range(reach)] for g in (-1, 0, 1)]
+    none = jnp.int32(0)
+    greeted = (
+        n_tp - 1
+        + jnp.where(z > 0, pick(count[0]), none)
+        + pick(count[1])
+        + jnp.where(z + 1 < nz, pick(count[2]), none)
+    )
     def place(row):
         return lax.rem(t + lax.div(row, local), n_tp) * local + lax.rem(row, local)
 
@@ -163,12 +232,27 @@
     sin_t[:fold, :] = jnp.where(low_lanes, -sines, sin_r)
     sin_t[fold:, :] = jnp.where(low_lanes, -sin_r, sines)
 
+    pl.semaphore_wait(barrier, greeted)
+
+    cuts = (0, width // 256 * 128, width)
+
+    def gather(w, j, n):
+        src, dst = (tokens, xg) if w == 0 else (rgrad, gg)
+        cols = slice(cuts[n], cuts[n + 1])
+        return to_tp(src.at[:, cols], dst.at[n_tp - j, :, cols], ag_send,
+                     ag_recv.at[w, j - 1, n], lax.rem(t + j, n_tp))
+
+    for w in range(2):
+        for n in range(2):
+            for j in range(1, n_tp):
+                gather(w, j, n).start()
+
     spans = (slice(0, local), slice(local, rows))
     chunks = [(w, i) for w in range(2) for i in range(2)]
 
     def key_values(w, x):
         span = spans[w]
-        raw[span, qc : qc + 2 * kc] = dot(x, wqkv[:, qc : qc + 2 * kc], 1, 0)
+        raw[span, qc : qc + 2 * kc] = x
         for m in range(kv_count):
             u = raw[span, qc + m * head : qc + (m + 1) * head]
             n = u * inverse_rms(u) * kgain[...]
@@ -176,63 +260,59 @@
             v0 = qc + kc + m * head
             kv_own[1, m, span] = raw[span, v0 : v0 + head].astype(bf16)
 
-    def hop(a, b, d, w, i):
-        span, e = spans[w], d + b - a
+    def hop(a, b, g, d, w, i):
+        span, e = spans[w], d + step_of(a, b, g)
         src = kv_own.at[i, :, span] if d == 0 else halo.at[d - 1, i, :, span]
-        return to_ctx(src, halo.at[e - 1, i, :, span], f_send.at[int(d > a)],
-                      f_recv.at[e - 1, w, i], c + b - a)
-
-    def ahead(w, i):
-        span = spans[w]
-        return to_ctx(kv_own.at[i, :, span], halo.at[reach - 1, i, :, span],
-                      f_send.at[2], f_recv.at[reach - 1, w, i], c + reach)
+        kind = 2 if g else int(d > a)
+        return to_ctx(src, halo.at[e - 1, i, :, span], f_send.at[kind],
+                      f_recv.at[e - 1, w, i], c + step_of(a, b, g))
 
     def arrived(d, w, i):
         span = spans[w]
         to_ctx(kv_own.at[i, :, span], halo.at[d - 1, i, :, span], f_send.at[2],
                f_recv.at[d - 1, w, i], c).wait_recv()
 
-    def at(k, a, d):
-        return (s == k) & (z > 0) if d > a else s == k
-
-    def relay(jobs):
-        for k in range(reach):
-            for early in (True, False):
-                mine = [j for j in jobs if j[0] == k and (j[1] > k) == early]
-                if mine:
-                    @pl.when((s == k) & (z > 0) if early else s == k)
-                    def _(mine=mine):
-                        for a, d, w in mine:
-                            for i in range(2):
-                                arrived(d, w, i)
-                                for b, ws in [(b, ws) for x, b, e, ws in TREE if (x, e) == (a, d)]:
-                                    if w in ws:
-                                        hop(a, b, d, w, i).start()
+    settled = set()
+
+    def settle(jobs):
+        for k, d, w in jobs:
+            if (k, d, w) in settled:
+                continue
+            settled.add((k, d, w))
+
+            @pl.when(here(k, early=d > k))
+            def _(k=k, d=d, w=w):
+                for i in range(2):
+                    arrived(d, w, i)
+                    for b, g in out_of(k, d, w):
+                        hop(k, b, g, d, w, i).start()
 
     for w in range(2):
         if w == 0:
             loads[0].wait()
             local_copy(4, wqkv.at[:, qc:], wqkv.at[:, qc:]).wait()
-            key_values(w, xg[0])
+            key_values(w, dot(xg[0], wqkv[:, qc:], 1, 0))
         else:
-            for j in range(1, n_tp):
-                gather(0, j).wait_recv()
-            key_values(w, xg[1:].reshape(rows - local, width))
-
-        @pl.when(z + 1 < nz)
-        def _(w=w):
-            for i in range(2):
-                ahead(w, i).start()
-
-        for k in range(reach - 1):
-            @pl.when(s == k)
-            def _(k=k, w=w):
-                for i in range(2):
-                    for b, _, _ in children(k, 0, w):
-                        hop(k, b, 0, w, i).start()
-
-    for j in range(1, n_tp):
-        gather(1, j).start()
+            projected = None
+            for n in range(2):
+                cols = slice(cuts[n], cuts[n + 1])
+                for j in range(1, n_tp):
+                    gather(0, j, n).wait_recv()
+                x = xg[1:, :, cols].reshape(rows - local, cuts[n + 1] - cuts[n])
+                piece = dot(x, wqkv[cols, qc:], 1, 0)
+                projected = piece if n == 0 else projected + piece
+            key_values(w, projected)
+
+        for k in range(reach):
+            for ahead in (1, 0):
+                targets = [b for b, g in out_of(k, 0, w) if g == ahead]
+                if targets:
+                    @pl.when(here(k, later=ahead > 0))
+                    def _(k=k, w=w, ahead=ahead, targets=targets):
+                        for b in targets:
+                            for i in range(2):
+                                hop(k, b, ahead, 0, w, i).start()
+
     loads[1].wait()
     raw[:, :qc] = dot(xg[...].reshape(rows, width), wqkv[:, :qc], 1, 0)
     for h in range(kv_count * per_kv):
@@ -240,19 +320,20 @@
         u = raw[:, h * head : (h + 1) * head]
         n = u * inverse_rms(u) * qgain[...]
         q_s[m, g * rows : (g + 1) * rows] = rope(n, cos_t[...], sin_t[...], half).astype(bf16)
-    relay([(1, 4, 0), (2, 4, 0), (3, 4, 0), (1, 1, 0), (3, 2, 0)])
+    settle(PASS_ON[0])
 
     loads[2].wait()
     loads[3].wait()
     for j in range(1, n_tp):
-        gather(1, j).wait_recv()
+        for n in range(2):
+            gather(1, j, n).wait_recv()
     d_out = dot(gg[...].reshape(rows, width), wo[...], 1, 1).astype(bf16)
     for h in range(kv_count * per_kv):
         m, g = h // per_kv, h % per_kv
         piece = d_out[:, h * head : (h + 1) * head]
         do_s[m, g * rows : (g + 1) * rows] = piece
         dot_s[m, :, g * rows : (g + 1) * rows] = piece.astype(f32).T
-    relay([(1, 4, 1), (2, 4, 1), (3, 4, 1), (2, 2, 1), (3, 2, 1)])
+    settle(PASS_ON[1])
 
     def kv(d, w, m):
         return kv_own[w, m] if isinstance(d, int) and d == 0 else halo[d - 1, w, m]
@@ -261,13 +342,15 @@
         for m in range(kv_count):
             key, value = kv(d, 0, m), kv(d, 1, m)
             e = jnp.exp(dot(key, q_s[m], 1, 1) * score_scale)
+            key_row = place(lax.broadcasted_iota(jnp.int32, (rows, 1), 0))
+            query_row = place(
+                lax.rem(lax.broadcasted_iota(jnp.int32, (1, qn), 1), jnp.int32(rows))
+            )
             if isinstance(d, int):
-                key_row = place(lax.broadcasted_iota(jnp.int32, (rows, 1), 0))
-                query_row = place(
-                    lax.rem(lax.broadcasted_iota(jnp.int32, (1, qn), 1), jnp.int32(rows))
-                )
-                keep = query_row >= key_row if d == 0 else query_row < key_row
-                e = jnp.where(keep, e, f32(0.0))
+                keep = query_row >= key_row
+            else:
+                keep = query_row < key_row + jnp.where(d == reach, 0, rows)
+            e = jnp.where(keep, e, f32(0.0))
             total = jnp.sum(e, axis=0, keepdims=True)
             low = e.astype(bf16)
             e_s[d, m] = low
@@ -281,43 +364,19 @@
                 ot_s[m] += mixed
 
     first_pass(0)
-    relay([(1, 2, 0), (0, 2, 0)])
-
-    @pl.when(z > 0)
-    def _():
-        for k in (0,):
-            @pl.when(s == k)
-            def _():
-                for w, i in chunks:
-                    arrived(reach, w, i)
-        first_pass(reach)
-
-    relay([(2, 3, 1), (0, 2, 1)])
-
-    def pick(*by_place):
-        value = jnp.int32(by_place[0])
-        for k in range(1, reach):
-            value = jnp.where(s == k, jnp.int32(by_place[k]), value)
-        return value
-
-    relayed = {(1, 4, 0), (2, 4, 0), (3, 4, 0), (1, 1, 0), (3, 2, 0), (1, 4, 1), (2, 4, 1), (3, 4, 1),
-               (2, 2, 1), (3, 2, 1), (1, 2, 0), (0, 2, 0), (2, 3, 1), (0, 2, 1)}
-    order = ((3, 2, 1), (1, 2, 3), (2, 1, 3), (1, 2, 3))
-    for step in range(reach - 1):
+
+    settle(PASS_ON[2])
+    for step in range(reach):
         for k in range(reach):
-            d = order[k][step]
-
-            @pl.when((s == k) & (z > 0) if d > k else s == k)
-            def _(k=k, d=d):
-                for w, i in chunks:
-                    if (k, d, w) not in relayed:
-                        arrived(d, w, i)
-
-        far = pick(*[order[k][step] for k in range(reach)])
+            settle([(k, FIRST[k][step], w) for w in range(2)])
+        far = pick([order[step] for order in FIRST])
 
         @pl.when(c >= far)
         def _(far=far):
             first_pass(far)
+
+        if step < 2:
+            settle(PASS_ON[3 + step])
 
     inv, delta = [], []
     for m in range(kv_count):
@@ -339,47 +398,45 @@
 
     def give(k, d, w, i):
         span = spans[w]
-        if d == reach:
-            return to_ctx(dkv.at[d - 1, i, :, span], gin.at[0, 2, i, :, span],
-                          b_send.at[1], b_recv.at[slot(k, 0, 2, w), i], c - reach)
-        a, e, axis = parent(k, d, w)
-        return to_ctx(dkv.at[d - 1, i, :, span], gin.at[e, axis, i, :, span],
-                      b_send.at[int(d > k)], b_recv.at[slot(a, e, axis, w), i], c + a - k)
-
-    def taken(k, d, axis, w, i):
+        b, g = home_of(k, d, w)
+        n = inbound(b).index((k, d, g, w))
+        return to_ctx(dkv.at[d - 1, i, :, span], gin.at[n, i, :, span],
+                      b_send.at[int(d > k)], b_recv.at[n, i], c + step_of(k, b, g))
+
+    def taken(k, giver, w, i):
         span = spans[w]
-        to_ctx(dkv.at[0, i, :, span], gin.at[d, axis, i, :, span], b_send.at[0],
-               b_recv.at[slot(k, d, axis, w), i], c).wait_recv()
-        return gin[d, axis, i, :, span].astype(f32)
+        n = inbound(k).index((*giver, w))
+        to_ctx(dkv.at[0, i, :, span], gin.at[n, i, :, span], b_send.at[0],
+               b_recv.at[n, i], c).wait_recv()
+        return gin[n, i, :, span].astype(f32)
 
     def combine(jobs):
-        for k in range(reach):
-            for early in (True, False):
-                mine = [j for j in jobs if j[0] == k and (j[1] > k) == early]
-                if mine:
-                    @pl.when((s == k) & (z > 0) if early else s == k)
-                    def _(mine=mine):
-                        for k, d, w in mine:
-                            for i in range(2):
-                                span = spans[w]
-                                total = dkv[d - 1, i, :, span].astype(f32)
-                                for _, _, axis in children(k, d, w):
-                                    total += taken(k, d, axis, w, i)
-                                dkv[d - 1, i, :, span] = total.astype(bf16)
-                                give(k, d, w, i).start()
-
-    for d in (1, 3, 2, 4):
-        @pl.when(c >= d)
-        def _(d=d):
+        for k, d, w in jobs:
+            @pl.when(here(k, early=d > k))
+            def _(k=k, d=d, w=w):
+                span = spans[w]
+                for i in range(2):
+                    total = dkv[d - 1, i, :, span].astype(f32)
+                    for giver in givers(k, d, w):
+                        total += taken(k, giver, w, i)
+                    dkv[d - 1, i, :, span] = total.astype(bf16)
+                    give(k, d, w, i).start()
+
+    for step in range(reach):
+        far = pick([order[step] for order in SECOND])
+
+        @pl.when(c >= far)
+        def _(step=step, far=far):
             for m in range(kv_count):
-                dk, dv = second_pass(d, m)
-                dkv[d - 1, 0, m] = dk.astype(bf16)
-                dkv[d - 1, 1, m] = dv.astype(bf16)
+                dk, dv = second_pass(far, m)
+                dkv[far - 1, 0, m] = dk.astype(bf16)
+                dkv[far - 1, 1, m] = dv.astype(bf16)
             for k in range(reach):
-                leaves = [w for w in (1, 0) if not children(k, d, w)]
+                d = SECOND[k][step]
+                leaves = [v for a, _, _, e, v in HOME if (a, e) == (k, d) and not givers(k, d, v)]
                 if leaves:
-                    @pl.when(s == k)
-                    def _(k=k, leaves=leaves):
+                    @pl.when(here(k))
+                    def _(k=k, d=d, leaves=leaves):
                         for w in leaves:
                             for i in range(2):
                                 give(k, d, w, i).start()
@@ -408,7 +465,9 @@
                 part[w, j, :, lo:hi] = both[j * local : (j + 1) * local].astype(bf16)
                 rs_copy(w, j, n).start()
 
+    combine(ADD_UP[0])
     project(0, att[...], xg, 0, qc, True)
+    combine(ADD_UP[1])
     for m in range(kv_count):
         for g in range(per_kv):
             h = m * per_kv + g
@@ -417,11 +476,9 @@
             back[:, h * head : (h + 1) * head] = norm_rope_back(
                 grad, u, qgain[...], cos_t[...], sin_t[...], half
             ).astype(bf16)
-    combine([(0, 2, 1), (0, 2, 0), (2, 3, 1), (2, 2, 1), (3, 2, 1), (3, 2, 0),
-             (1, 2, 0), (1, 4, 1), (1, 4, 0), (1, 1, 0)])
+    combine(ADD_UP[2])
     project(1, back[:, :qc], gg, 0, qc, False)
-    combine([(2, 4, 1), (2, 4, 0), (3, 4, 1), (3, 4, 0)])
-
+    combine(ADD_UP[3])
     def landed(w, n):
         lo, hi = tiles[n]
         total = acc[w if w < 2 else 1, :, lo:hi]
@@ -432,6 +489,7 @@
 
     for n, (lo, hi) in enumerate(tiles):
         out_ref[:, lo:hi] = landed(0, n).astype(bf16)
+    combine(ADD_UP[4])
     for n, (lo, hi) in enumerate(tiles):
         acc[1, :, lo:hi] = landed(1, n)
 
@@ -439,16 +497,13 @@
         span = spans[w]
         for i in range(2):
             for k in range(reach):
-                kids = children(k, 0, w)
-                if kids:
-                    @pl.when(s == k)
-                    def _(kids=kids, w=w, i=i, span=span, k=k):
-                        for _, _, axis in kids:
-                            own_grad[i, :, span] += taken(k, 0, axis, w, i)
-
-            @pl.when(z + 1 < nz)
-            def _(w=w, i=i, span=span):
-                own_grad[i, :, span] += taken(0, 0, 2, w, i)
+                for later in (False, True):
+                    mine = [x for x in givers(k, 0, w) if bool(x[2]) == later]
+                    if mine:
+                        @pl.when(here(k, later=later))
+                        def _(k=k, mine=mine, w=w, i=i, span=span):
+                            for giver in mine:
+                                own_grad[i, :, span] += taken(k, giver, w, i)
 
         for m in range(kv_count):
             k0 = qc + m * head
@@ -475,22 +530,25 @@
     sent(ag_send, part.at[:2, 1:])
     sent(rs_send, part.at[:, 1:])
 
-    @pl.when(z + 1 < nz)
-    def _():
-        sent(f_send.at[2], kv_own)
+    def drain(sem, ref, pieces):
+        few = [pieces.count(w) for w in range(2)]
+        both = min(few)
+        if both:
+            sent(sem, ref.at[:both])
+        for w in range(2):
+            if few[w] > both:
+                sent(sem, ref.at[: few[w] - both, :, :, spans[w]])
 
     for k in range(reach):
-        for early in (True, False):
-            @pl.when((s == k) & (z > 0) if early else s == k)
-            def _(k=k, early=early):
-                halves = sum(len(ws) for a, b, d, ws in TREE if a == k and (d > k) == early)
-                if halves // 2:
-                    sent(f_send.at[int(early)], halo.at[: halves // 2])
-                if halves % 2:
-                    sent(f_send.at[int(early)], halo.at[0, :, :, spans[0]])
-                first, last = (k, reach) if early else (0, k)
-                if first < last:
-                    sent(b_send.at[int(early)], dkv.at[first:last])
+        for kind in range(3):
+            gone = [v for a, b, g, e, v in OUT if a == k and kind == (2 if g else int(e > a))]
+            back_gone = [v for a, b, g, e, v in HOME if a == k and kind == int(e > a)]
+            if gone or back_gone:
+                @pl.when(here(k, early=kind == 1, later=kind == 2))
+                def _(kind=kind, gone=gone, back_gone=back_gone):
+                    drain(f_send.at[kind], halo, gone)
+                    if kind < 2:
+                        drain(b_send.at[kind], dkv, back_gone)
 
 
 def write(a, b, a_out, b_out, sems):
@@ -518,7 +576,7 @@
     kv_count = key_weight.shape[1] // head
     per_kv = query_weight.shape[1] // key_weight.shape[1]
     reach = WINDOW // rows
-    assert reach == 4 and n_ctx % reach == 0
+    assert reach == GROUP and n_ctx % reach == 0
     qc = kv_count * per_kv * head
     kc = kv_count * head
     qn = per_kv * rows
@@ -557,7 +615,7 @@
             pltpu.VMEM((rows, qc), bf16),
             pltpu.VMEM((reach,) + block, bf16),
             pltpu.VMEM(block, f32),
-            pltpu.VMEM((reach + 1, 3) + block, bf16),
+            pltpu.VMEM((SLOTS,) + block, bf16),
             pltpu.VMEM((rows, qc + 2 * kc), bf16),
             pltpu.VMEM((3, n_tp, local, width), bf16),
             pltpu.VMEM((3, n_tp - 1, local, width), bf16),
@@ -565,7 +623,7 @@
             pltpu.VMEM((3, 1, head), f32),
             dma((6,)),
             dma,
-            dma((2, n_tp - 1)),
+            dma((2, n_tp - 1, 2)),
             dma((3,)),
             dma((reach, 2, 2)),
             dma((2,)),

time: 31.1 us -> 26.7 us (0.86)
  the two profiles are of different devices: /device:TPU:15 before, /device:TPU:0 now
where the time goes in v2:
time: 26.7 us; the launch traced here: 26.4 us
  Pallas kernels  25.7 us (96%)
  between operations  0.64 us (2%)
    pallas_call x1, Pallas kernels, on_device(): pl.pallas_call(functools.partial(kernel, n_ctx, n_tp, reach, per_kv, kv_c...  24.6 us
    pallas_call x1, Pallas kernels, on_device(): pl.pallas_call(write, out_shape=(result, result), in_specs=[vmem_spec] *...  1.14 us

profile of v2, /device:TPU:0, one launch (start us, length us, event | category | flops | bytes accessed | tf_op | source)
XLA Modules:
  0.0 26.4 jit_solution(2129831171863147191)
XLA Ops:
  0.6 24.6 %shard_map.104 = (bf16[128,2688]{1,0:T(8,128)(2,1)S(1)}, bf16[128,2688]{1,0:T(8,128)(2,1)S(1)}) custom-call(bf16[128,2688]{1,0:T(8,128)(2,1)} %tokens.1, bf16[128,2688]{1,0:T(8,128)(2,1)} %rgrad.1, bf16[2688,256]{1,0:T(8,128)(2,1)} %qw.1, bf16[2688,128]{1,0:T(8,128)(2,1)} %kw.1, bf16[2688,128]{1,0:T(8,128)(2,1)} %vw.1, bf16[256,2688]{1,0:T(8,128)(2,1)} %ow.1, ...), custom_call_target="tpu_custom_call" | custom-call | tf_op jit(solution)/shard_map/pallas_call | solution.py:592
  25.2 1.1 %shard_map.105 = (bf16[128,2688]{1,0:T(8,128)(2,1)}, bf16[128,2688]{1,0:T(8,128)(2,1)}) custom-call(bf16[128,2688]{1,0:T(8,128)(2,1)S(1)} %get-tuple-element.4.a, bf16[128,2688]{1,0:T(8,128)(2,1)S(1)} %get-tuple-element.5.b), custom_call_target="tpu_custom_call" | custom-call | tf_op jit(solution)/shard_map/pallas_call | solution.py:642

commit v3 on v2

--- a/solution.py
+++ b/solution.py
@@ -13,35 +13,41 @@
 score_scale = 168.0 ** (-0.5)
 rope_theta = 10000.0
 MESH = pl.DeviceIdType.MESH
-TREE = (
-    (0, 1, 0, (0, 1)), (0, 2, 0, (0, 1)), (1, 3, 0, (0, 1)), (2, 3, 0, (0, 1)),
-    (1, 0, 4, (0, 1)), (2, 0, 4, (0, 1)), (3, 2, 4, (0, 1)), (3, 1, 4, (0, 1)),
-    (1, 3, 1, (0,)), (2, 3, 2, (1,)), (3, 2, 2, (0, 1)),
-    (1, 0, 2, (0,)), (2, 0, 3, (1,)), (0, 1, 2, (0, 1)),
-)
 OUT = (
-    (0, 0, 1, 0, 0), (1, 3, 0, 0, 0), (2, 3, 0, 0, 0), (1, 1, 1, 0, 0), (0, 2, 0, 0, 0),
-    (3, 2, 1, 0, 0), (1, 2, 0, 0, 0), (1, 0, 1, 0, 0), (0, 1, 0, 0, 0), (2, 0, 1, 0, 0),
-    (0, 2, 0, 0, 1), (0, 1, 0, 0, 1), (2, 3, 0, 0, 1), (1, 0, 1, 0, 1), (0, 0, 1, 0, 1),
-    (3, 1, 1, 0, 1), (1, 1, 1, 0, 1), (2, 0, 1, 0, 1), (2, 2, 1, 0, 1), (1, 3, 0, 0, 1),
-    (3, 2, 1, 0, 1), (3, 3, 1, 0, 1), (1, 3, 0, 1, 0), (2, 0, 0, 3, 0), (2, 1, 0, 3, 0),
-    (0, 1, 0, 2, 0), (0, 2, 0, 2, 0), (2, 3, 0, 3, 0), (1, 3, 0, 1, 1), (3, 2, 0, 2, 1),
-    (0, 1, 0, 2, 1), (1, 0, 0, 2, 1),
+    (0, 0, 1, 0, 0, 0), (0, 0, 1, 0, 0, 1), (1, 3, 0, 0, 0, 0), (1, 3, 0, 0, 0, 1), (2, 3, 0, 0, 0, 0),
+    (2, 3, 0, 0, 0, 1), (1, 1, 1, 0, 0, 0), (1, 1, 1, 0, 0, 1), (0, 2, 0, 0, 0, 0), (0, 2, 0, 0, 0, 1),
+    (3, 2, 1, 0, 0, 0), (3, 2, 1, 0, 0, 1), (1, 2, 0, 0, 0, 0), (1, 2, 0, 0, 0, 1), (1, 0, 1, 0, 0, 0),
+    (1, 0, 1, 0, 0, 1), (0, 1, 0, 0, 0, 0), (0, 1, 0, 0, 0, 1), (2, 0, 1, 0, 0, 0), (2, 0, 1, 0, 0, 1),
+    (0, 2, 0, 0, 1, 0), (0, 2, 0, 0, 1, 1), (0, 1, 0, 0, 1, 0), (0, 1, 0, 0, 1, 1), (2, 3, 0, 0, 1, 0),
+    (2, 3, 0, 0, 1, 1), (1, 0, 1, 0, 1, 0), (1, 0, 1, 0, 1, 1), (0, 0, 1, 0, 1, 0), (0, 0, 1, 0, 1, 1),
+    (3, 1, 1, 0, 1, 0), (3, 1, 1, 0, 1, 1), (1, 1, 1, 0, 1, 0), (1, 1, 1, 0, 1, 1), (2, 0, 1, 0, 1, 0),
+    (2, 0, 1, 0, 1, 1), (2, 2, 1, 0, 1, 0), (2, 2, 1, 0, 1, 1), (1, 3, 0, 0, 1, 0), (1, 3, 0, 0, 1, 1),
+    (3, 2, 1, 0, 1, 0), (3, 2, 1, 0, 1, 1), (3, 3, 1, 0, 1, 0), (3, 3, 1, 0, 1, 1), (1, 3, 0, 1, 0, 0),
+    (2, 0, 0, 3, 0, 0), (2, 1, 0, 3, 0, 0), (0, 1, 0, 2, 0, 0), (0, 2, 0, 2, 0, 0), (2, 3, 0, 3, 0, 0),
+    (1, 3, 0, 1, 0, 1), (2, 0, 0, 3, 0, 1), (2, 1, 0, 3, 0, 1), (0, 1, 0, 2, 0, 1), (0, 2, 0, 2, 0, 1),
+    (2, 3, 0, 3, 0, 1), (1, 3, 0, 1, 1, 0), (3, 2, 0, 2, 1, 0), (0, 1, 0, 2, 1, 0), (1, 0, 0, 2, 1, 0),
+    (1, 3, 0, 1, 1, 1), (3, 2, 0, 2, 1, 1), (0, 1, 0, 2, 1, 1), (1, 0, 0, 2, 1, 1),
 )
 HOME = (
-    (1, 0, 0, 3, 1), (3, 3, -1, 4, 0), (3, 0, 0, 3, 0), (1, 1, -1, 4, 0), (0, 2, 0, 1, 1),
-    (3, 2, 0, 1, 1), (0, 0, -1, 4, 1), (0, 1, 0, 3, 1), (2, 3, -1, 3, 1), (2, 1, 0, 1, 1),
-    (1, 0, 0, 1, 0), (2, 3, 0, 1, 0), (3, 1, 0, 2, 0), (0, 0, -1, 4, 0), (1, 0, 0, 1, 1),
-    (3, 1, 0, 2, 1), (2, 2, -1, 4, 0), (0, 1, 0, 3, 0), (3, 2, 0, 1, 0), (1, 1, -1, 4, 1),
-    (3, 2, 0, 4, 1), (0, 2, -1, 2, 0), (0, 2, 0, 1, 0), (0, 2, -1, 2, 1), (1, 0, 0, 3, 0),
-    (2, 3, -1, 3, 0), (1, 3, -1, 2, 1), (2, 0, 0, 2, 0), (1, 3, -1, 2, 0), (2, 2, -1, 4, 1),
-    (3, 1, 0, 3, 1), (2, 0, 0, 2, 1),
+    (1, 0, 0, 3, 1, 0), (1, 0, 0, 3, 1, 1), (3, 3, -1, 4, 0, 0), (3, 3, -1, 4, 0, 1), (3, 0, 0, 3, 0, 0),
+    (3, 0, 0, 3, 0, 1), (1, 1, -1, 4, 0, 0), (1, 1, -1, 4, 0, 1), (0, 2, 0, 1, 1, 0), (0, 2, 0, 1, 1, 1),
+    (3, 2, 0, 1, 1, 0), (3, 2, 0, 1, 1, 1), (0, 0, -1, 4, 1, 0), (0, 0, -1, 4, 1, 1), (0, 1, 0, 3, 1, 0),
+    (0, 1, 0, 3, 1, 1), (2, 3, -1, 3, 1, 0), (2, 3, -1, 3, 1, 1), (2, 1, 0, 1, 1, 0), (2, 1, 0, 1, 1, 1),
+    (1, 0, 0, 1, 0, 0), (1, 0, 0, 1, 0, 1), (2, 3, 0, 1, 0, 0), (2, 3, 0, 1, 0, 1), (3, 1, 0, 2, 0, 0),
+    (3, 1, 0, 2, 0, 1), (0, 0, -1, 4, 0, 0), (0, 0, -1, 4, 0, 1), (1, 0, 0, 1, 1, 0), (1, 0, 0, 1, 1, 1),
+    (3, 1, 0, 2, 1, 0), (3, 1, 0, 2, 1, 1), (2, 2, -1, 4, 0, 0), (0, 1, 0, 3, 0, 0), (2, 2, -1, 4, 0, 1),
+    (0, 1, 0, 3, 0, 1), (3, 2, 0, 1, 0, 0), (3, 2, 0, 1, 0, 1), (1, 1, -1, 4, 1, 0), (1, 1, -1, 4, 1, 1),
+    (3, 2, 0, 4, 1, 0), (3, 2, 0, 4, 1, 1), (0, 2, -1, 2, 0, 0), (0, 2, -1, 2, 0, 1), (0, 2, 0, 1, 0, 0),
+    (0, 2, 0, 1, 0, 1), (0, 2, -1, 2, 1, 0), (0, 2, -1, 2, 1, 1), (1, 0, 0, 3, 0, 0), (1, 0, 0, 3, 0, 1),
+    (2, 3, -1, 3, 0, 0), (2, 3, -1, 3, 0, 1), (1, 3, -1, 2, 1, 0), (1, 3, -1, 2, 1, 1), (2, 0, 0, 2, 0, 0),
+    (2, 0, 0, 2, 0, 1), (1, 3, -1, 2, 0, 0), (1, 3, -1, 2, 0, 1), (2, 2, -1, 4, 1, 0), (2, 2, -1, 4, 1, 1),
+    (3, 1, 0, 3, 1, 0), (3, 1, 0, 3, 1, 1), (2, 0, 0, 2, 1, 0), (2, 0, 0, 2, 1, 1),
 )
 PASS_ON = (
-    (), ((1, 1, 0), (0, 2, 0), (2, 3, 0)), ((1, 1, 1), (3, 2, 1)), ((0, 2, 1), (1, 2, 1)), (),
+    ((1, 1, 0, 0), (0, 2, 0, 0), (2, 3, 0, 0)), ((1, 1, 0, 1), (0, 2, 0, 1), (2, 3, 0, 1), (1, 1, 1, 0), (3, 2, 1, 0), (0, 2, 1, 0), (1, 2, 1, 0)), ((1, 1, 1, 1), (3, 2, 1, 1)), ((0, 2, 1, 1), (1, 2, 1, 1)), (),
 )
 ADD_UP = (
-    (), (), ((0, 2, 1), (2, 3, 1)), ((1, 4, 1), (0, 2, 0)), ((1, 1, 1), (2, 3, 0), (3, 2, 0), (1, 4, 0)),
+    (), ((0, 2, 1, 0), (1, 1, 1, 0), (2, 3, 1, 0)), ((0, 2, 1, 1), (1, 4, 1, 0), (2, 3, 1, 1)), ((0, 2, 0, 0), (1, 4, 1, 1), (2, 3, 0, 0), (3, 2, 0, 0), (0, 2, 0, 1)), ((1, 4, 0, 0), (1, 1, 1, 1), (2, 3, 0, 1), (3, 2, 0, 1), (1, 4, 0, 1)),
 )
 FIRST = ((4, 2, 3, 1), (1, 2, 4, 3), (2, 3, 4, 1), (2, 1, 4, 3))
 SECOND = ((4, 1, 3, 2), (3, 2, 1, 4), (4, 1, 2, 3), (4, 3, 1, 2))
@@ -72,55 +78,32 @@
     return r * (w - u * (r * r * jnp.mean(w * u, axis=-1, keepdims=True)))
 
 
-def axis_of(a, b):
-    return 0 if a ^ b == 1 else 1
-
-
-def children(place, d, w):
-    return [(b, d + b - a, axis_of(a, b)) for a, b, e, ws in TREE if (a, e) == (place, d) and w in ws]
-
-
-def parent(place, d, w):
-    (a,) = [(a, e, axis_of(a, b)) for a, b, e, ws in TREE if (b, e + b - a) == (place, d) and w in ws]
-    return a
-
-
-def slot(place, d, axis, w):
-    if axis == 2:
-        return w
-    seen = [(e, axis_of(a, b), v) for a, b, e, ws in TREE if a == place for v in ws]
-    return 2 + seen.index((d, axis, w))
-
-
-SLOTS = 2 + max(sum(len(ws) for a, _, _, ws in TREE if a == place) for place in range(4))
-
-
 def step_of(a, b, ahead):
     return GROUP * ahead + b - a
 
 
-def out_of(place, d, w):
-    return [(b, g) for a, b, g, e, v in OUT if (a, e, v) == (place, d, w)]
-
-
-def home_of(place, d, w):
-    ((b, g),) = [(b, g) for a, b, g, e, v in HOME if (a, e, v) == (place, d, w)]
+def out_of(place, d, w, i):
+    return [(b, g) for a, b, g, *piece in OUT if (a, *piece) == (place, d, w, i)]
+
+
+def home_of(place, d, w, i):
+    ((b, g),) = [(b, g) for a, b, g, *piece in HOME if (a, *piece) == (place, d, w, i)]
     return b, g
 
 
 def inbound(place):
-    return [(a, e, g, v) for a, b, g, e, v in HOME if b == place]
-
-
-def givers(place, d, w):
+    return [(a, e, g, w, i) for a, b, g, e, w, i in HOME if b == place]
+
+
+def givers(place, d, w, i):
     return [
-        (a, e, g) for a, e, g, v in inbound(place)
-        if v == w and e + step_of(a, place, g) == d
+        (a, e, g) for a, e, g, *piece in inbound(place)
+        if piece == [w, i] and e + step_of(a, place, g) == d
     ]
 
 
 def partners(place, g):
-    pairs = {(a, b, h) for a, b, h, _, _ in OUT + HOME}
+    pairs = {edge[:3] for edge in OUT + HOME}
     pairs |= {(b, a, -h) for a, b, h in pairs}
     return sorted(b for a, b, h in pairs if (a, h) == (place, g) and (b, g) != (place, 0))
 
@@ -192,7 +175,7 @@
         local_copy(4, vw, wqkv.at[:, qc + kc : qc + 2 * kc]),
     ]
     table_loads = [local_copy(5, x, rope_in.at[i]) for i, x in enumerate((freq_in, kgain_in, qgain_in))]
-    for load in table_loads + loads[:1] + kv_loads + loads[1:]:
+    for load in table_loads + loads[:1] + kv_loads + loads[2:3] + loads[1:2] + loads[3:]:
         load.start()
 
     def to_ctx(src, dst, send, recv, target):
@@ -232,21 +215,6 @@
     sin_t[:fold, :] = jnp.where(low_lanes, -sines, sin_r)
     sin_t[fold:, :] = jnp.where(low_lanes, -sin_r, sines)
 
-    pl.semaphore_wait(barrier, greeted)
-
-    cuts = (0, width // 256 * 128, width)
-
-    def gather(w, j, n):
-        src, dst = (tokens, xg) if w == 0 else (rgrad, gg)
-        cols = slice(cuts[n], cuts[n + 1])
-        return to_tp(src.at[:, cols], dst.at[n_tp - j, :, cols], ag_send,
-                     ag_recv.at[w, j - 1, n], lax.rem(t + j, n_tp))
-
-    for w in range(2):
-        for n in range(2):
-            for j in range(1, n_tp):
-                gather(w, j, n).start()
-
     spans = (slice(0, local), slice(local, rows))
     chunks = [(w, i) for w in range(2) for i in range(2)]
 
@@ -275,43 +243,63 @@
     settled = set()
 
     def settle(jobs):
-        for k, d, w in jobs:
-            if (k, d, w) in settled:
+        for k, d, w, i in jobs:
+            if (k, d, w, i) in settled:
                 continue
-            settled.add((k, d, w))
+            settled.add((k, d, w, i))
 
             @pl.when(here(k, early=d > k))
-            def _(k=k, d=d, w=w):
-                for i in range(2):
-                    arrived(d, w, i)
-                    for b, g in out_of(k, d, w):
-                        hop(k, b, g, d, w, i).start()
-
-    for w in range(2):
-        if w == 0:
-            loads[0].wait()
-            local_copy(4, wqkv.at[:, qc:], wqkv.at[:, qc:]).wait()
-            key_values(w, dot(xg[0], wqkv[:, qc:], 1, 0))
-        else:
-            projected = None
-            for n in range(2):
-                cols = slice(cuts[n], cuts[n + 1])
-                for j in range(1, n_tp):
-                    gather(0, j, n).wait_recv()
-                x = xg[1:, :, cols].reshape(rows - local, cuts[n + 1] - cuts[n])
-                piece = dot(x, wqkv[cols, qc:], 1, 0)
-                projected = piece if n == 0 else projected + piece
-            key_values(w, projected)
-
+            def _(k=k, d=d, w=w, i=i):
+                arrived(d, w, i)
+                for b, g in out_of(k, d, w, i):
+                    hop(k, b, g, d, w, i).start()
+
+    pl.semaphore_wait(barrier, greeted)
+
+    cuts = (*range(0, width, 768), width)
+    pieces = len(cuts) - 1
+
+    def gather(w, j, n):
+        dst = xg if w == 0 else gg
+        cols = slice(cuts[n], cuts[n + 1]) if w == 0 else slice(None)
+        return to_tp(dst.at[0, :, cols], dst.at[n_tp - j, :, cols], ag_send,
+                     ag_recv.at[w * pieces + n, j - 1], lax.rem(t + j, n_tp))
+
+    loads[0].wait()
+    for n in range(pieces):
+        for j in range(1, n_tp):
+            gather(0, j, n).start()
+
+
+    local_copy(4, wqkv.at[:, qc:], wqkv.at[:, qc:]).wait()
+    key_values(0, dot(xg[0], wqkv[:, qc:], 1, 0))
+
+    def send_own(w):
         for k in range(reach):
             for ahead in (1, 0):
-                targets = [b for b, g in out_of(k, 0, w) if g == ahead]
+                targets = [
+                    (b, i) for a, b, g, d, v, i in OUT if (a, g, d, v) == (k, ahead, 0, w)
+                ]
                 if targets:
                     @pl.when(here(k, later=ahead > 0))
-                    def _(k=k, w=w, ahead=ahead, targets=targets):
-                        for b in targets:
-                            for i in range(2):
-                                hop(k, b, ahead, 0, w, i).start()
+                    def _(k=k, ahead=ahead, targets=targets):
+                        for b, i in targets:
+                            hop(k, b, ahead, 0, w, i).start()
+
+    send_own(0)
+    loads[2].wait()
+    for j in range(1, n_tp):
+        gather(1, j, 0).start()
+    projected = None
+    for n in range(pieces):
+        cols = slice(cuts[n], cuts[n + 1])
+        for j in range(1, n_tp):
+            gather(0, j, n).wait_recv()
+        x = xg[1:, :, cols].reshape(rows - local, cuts[n + 1] - cuts[n])
+        piece = dot(x, wqkv[cols, qc:], 1, 0)
+        projected = piece if n == 0 else projected + piece
+    key_values(1, projected)
+    send_own(1)
 
     loads[1].wait()
     raw[:, :qc] = dot(xg[...].reshape(rows, width), wqkv[:, :qc], 1, 0)
@@ -322,11 +310,9 @@
         q_s[m, g * rows : (g + 1) * rows] = rope(n, cos_t[...], sin_t[...], half).astype(bf16)
     settle(PASS_ON[0])
 
-    loads[2].wait()
     loads[3].wait()
     for j in range(1, n_tp):
-        for n in range(2):
-            gather(1, j, n).wait_recv()
+        gather(1, j, 0).wait_recv()
     d_out = dot(gg[...].reshape(rows, width), wo[...], 1, 1).astype(bf16)
     for h in range(kv_count * per_kv):
         m, g = h // per_kv, h % per_kv
@@ -368,7 +354,7 @@
     settle(PASS_ON[2])
     for step in range(reach):
         for k in range(reach):
-            settle([(k, FIRST[k][step], w) for w in range(2)])
+            settle([(k, FIRST[k][step], w, i) for w, i in chunks])
         far = pick([order[step] for order in FIRST])
 
         @pl.when(c >= far)
@@ -398,29 +384,27 @@
 
     def give(k, d, w, i):
         span = spans[w]
-        b, g = home_of(k, d, w)
-        n = inbound(b).index((k, d, g, w))
-        return to_ctx(dkv.at[d - 1, i, :, span], gin.at[n, i, :, span],
-                      b_send.at[int(d > k)], b_recv.at[n, i], c + step_of(k, b, g))
+        b, g = home_of(k, d, w, i)
+        n = inbound(b).index((k, d, g, w, i))
+        return to_ctx(dkv.at[d - 1, i, :, span], gin.at[n, :, span],
+                      b_send.at[int(d > k)], b_recv.at[n], c + step_of(k, b, g))
 
     def taken(k, giver, w, i):
         span = spans[w]
-        n = inbound(k).index((*giver, w))
-        to_ctx(dkv.at[0, i, :, span], gin.at[n, i, :, span], b_send.at[0],
-               b_recv.at[n, i], c).wait_recv()
-        return gin[n, i, :, span].astype(f32)
+        n = inbound(k).index((*giver, w, i))
+        to_ctx(dkv.at[0, i, :, span], gin.at[n, :, span], b_send.at[0], b_recv.at[n], c).wait_recv()
+        return gin[n, :, span].astype(f32)
 
     def combine(jobs):
-        for k, d, w in jobs:
+        for k, d, w, i in jobs:
             @pl.when(here(k, early=d > k))
-            def _(k=k, d=d, w=w):
+            def _(k=k, d=d, w=w, i=i):
                 span = spans[w]
-                for i in range(2):
-                    total = dkv[d - 1, i, :, span].astype(f32)
-                    for giver in givers(k, d, w):
-                        total += taken(k, giver, w, i)
-                    dkv[d - 1, i, :, span] = total.astype(bf16)
-                    give(k, d, w, i).start()
+                total = dkv[d - 1, i, :, span].astype(f32)
+                for giver in givers(k, d, w, i):
+                    total += taken(k, giver, w, i)
+                dkv[d - 1, i, :, span] = total.astype(bf16)
+                give(k, d, w, i).start()
 
     for step in range(reach):
         far = pick([order[step] for order in SECOND])
@@ -433,13 +417,15 @@
                 dkv[far - 1, 1, m] = dv.astype(bf16)
             for k in range(reach):
                 d = SECOND[k][step]
-                leaves = [v for a, _, _, e, v in HOME if (a, e) == (k, d) and not givers(k, d, v)]
+                leaves = [
+                    (w, i) for a, _, _, e, w, i in HOME
+                    if (a, e) == (k, d) and not givers(k, d, w, i)
+                ]
                 if leaves:
                     @pl.when(here(k))
                     def _(k=k, d=d, leaves=leaves):
-                        for w in leaves:
-                            for i in range(2):
-                                give(k, d, w, i).start()
+                        for w, i in leaves:
+                            give(k, d, w, i).start()
 
     for m in range(kv_count):
         dk, dv = second_pass(0, m)
@@ -449,7 +435,7 @@
     def rs_copy(w, j, n):
         cols = slice(*tiles[n])
         return to_tp(part.at[w, j, :, cols], rs_in.at[w, j - 1, :, cols], rs_send,
-                     rs_recv.at[w, j - 1, n], lax.rem(t + j, n_tp))
+                     rs_recv.at[w + n if w == 2 else w, j - 1], lax.rem(t + j, n_tp))
 
     def product(lhs, n, first, last, by_row):
         cols = slice(*tiles[n])
@@ -463,7 +449,11 @@
             acc[w, :, lo:hi] = base[0, :, lo:hi].astype(f32) + both[:local]
             for j in range(1, n_tp):
                 part[w, j, :, lo:hi] = both[j * local : (j + 1) * local].astype(bf16)
-                rs_copy(w, j, n).start()
+
+    def exchange(w):
+        for j in range(1, n_tp):
+            to_tp(part.at[w, j], rs_in.at[w, j - 1], rs_send, rs_recv.at[w, j - 1],
+                  lax.rem(t + j, n_tp)).start()
 
     combine(ADD_UP[0])
     project(0, att[...], xg, 0, qc, True)
@@ -477,28 +467,26 @@
                 grad, u, qgain[...], cos_t[...], sin_t[...], half
             ).astype(bf16)
     combine(ADD_UP[2])
+    exchange(0)
     project(1, back[:, :qc], gg, 0, qc, False)
     combine(ADD_UP[3])
-    def landed(w, n):
-        lo, hi = tiles[n]
-        total = acc[w if w < 2 else 1, :, lo:hi]
+    combine(ADD_UP[4])
+    exchange(1)
+    def landed(w):
         for j in range(1, n_tp):
-            rs_copy(w, j, n).wait_recv()
-            total += rs_in[w, j - 1, :, lo:hi].astype(f32)
-        return total
-
-    for n, (lo, hi) in enumerate(tiles):
-        out_ref[:, lo:hi] = landed(0, n).astype(bf16)
-    combine(ADD_UP[4])
-    for n, (lo, hi) in enumerate(tiles):
-        acc[1, :, lo:hi] = landed(1, n)
+            block = part.at[w, j]
+            to_tp(block, rs_in.at[w, j - 1], rs_send, rs_recv.at[w, j - 1], t).wait_recv()
+        return sum(rs_in[w, j - 1].astype(f32) for j in range(1, n_tp))
+
+    out_ref[...] = (acc[0] + landed(0)).astype(bf16)
+    acc[1] += landed(1)
 
     for w in (1, 0):
         span = spans[w]
         for i in range(2):
             for k in range(reach):
                 for later in (False, True):
-                    mine = [x for x in givers(k, 0, w) if bool(x[2]) == later]
+                    mine = [x for x in givers(k, 0, w, i) if bool(x[2]) == later]
                     if mine:
                         @pl.when(here(k, later=later))
                         def _(k=k, mine=mine, w=w, i=i, span=span):
@@ -522,7 +510,11 @@
                     part[2, j, :, lo:hi] = piece[(j - 1) * local : j * local].astype(bf16)
                     rs_copy(2, j, n).start()
     for n, (lo, hi) in enumerate(tiles):
-        gout_ref[:, lo:hi] = landed(2, n).astype(bf16)
+        total = acc[1, :, lo:hi]
+        for j in range(1, n_tp):
+            rs_copy(2, j, n).wait_recv()
+            total += rs_in[2, j - 1, :, lo:hi].astype(f32)
+        gout_ref[:, lo:hi] = total.astype(bf16)
 
     def sent(sem, ref):
         pltpu.make_async_copy(ref, ref, sem).wait()
@@ -531,18 +523,14 @@
     sent(rs_send, part.at[:, 1:])
 
     def drain(sem, ref, pieces):
-        few = [pieces.count(w) for w in range(2)]
-        both = min(few)
-        if both:
-            sent(sem, ref.at[:both])
-        for w in range(2):
-            if few[w] > both:
-                sent(sem, ref.at[: few[w] - both, :, :, spans[w]])
+        for w, i in chunks:
+            if pieces.count((w, i)):
+                sent(sem, ref.at[: pieces.count((w, i)), i, :, spans[w]])
 
     for k in range(reach):
         for kind in range(3):
-            gone = [v for a, b, g, e, v in OUT if a == k and kind == (2 if g else int(e > a))]
-            back_gone = [v for a, b, g, e, v in HOME if a == k and kind == int(e > a)]
+            gone = [(w, i) for a, _, g, e, w, i in OUT if a == k and kind == (2 if g else int(e > a))]
+            back_gone = [(w, i) for a, _, _, e, w, i in HOME if a == k and kind == int(e > a)]
             if gone or back_gone:
                 @pl.when(here(k, early=kind == 1, later=kind == 2))
                 def _(kind=kind, gone=gone, back_gone=back_gone):
@@ -552,17 +540,13 @@
 
 
 def write(a, b, a_out, b_out, sems):
-    split = sems.shape[1]
-    step = a.shape[0] // split
-    copies = [
-        pltpu.make_async_copy(x.at[pl.ds(i * step, step)], y.at[pl.ds(i * step, step)], sems.at[w, i])
-        for w, (x, y) in enumerate(((a, a_out), (b, b_out)))
-        for i in range(split)
-    ]
-    for copy in copies:
-        copy.start()
-    for copy in copies:
-        copy.wait()
+    rows = a.shape[0]
+    step = rows // 8 if rows % 64 == 0 else rows
+    for w, (x, y) in enumerate(((a, a_out), (b, b_out))):
+        for i in range(0, rows, step):
+            pltpu.make_async_copy(x.at[pl.ds(i, step)], y.at[pl.ds(i, step)], sems.at[w]).start()
+    for w, x in enumerate((a, b)):
+        pltpu.make_async_copy(x, x, sems.at[w]).wait()
 
 
 def on_device(
@@ -615,7 +599,7 @@
             pltpu.VMEM((rows, qc), bf16),
             pltpu.VMEM((reach,) + block, bf16),
             pltpu.VMEM(block, f32),
-            pltpu.VMEM((SLOTS,) + block, bf16),
+            pltpu.VMEM((SLOTS, kv_count, rows, head), bf16),
             pltpu.VMEM((rows, qc + 2 * kc), bf16),
             pltpu.VMEM((3, n_tp, local, width), bf16),
             pltpu.VMEM((3, n_tp - 1, local, width), bf16),
@@ -623,13 +607,13 @@
             pltpu.VMEM((3, 1, head), f32),
             dma((6,)),
             dma,
-            dma((2, n_tp - 1, 2)),
+            dma((pl.cdiv(width, 768) + 1, n_tp - 1)),
             dma((3,)),
             dma((reach, 2, 2)),
             dma((2,)),
-            dma((SLOTS, 2)),
+            dma((SLOTS,)),
             dma,
-            dma((3, n_tp - 1, len(tiles))),
+            dma((2 + len(tiles), n_tp - 1)),
         ],
         compiler_params=pltpu.CompilerParams(
             collective_id=0, has_side_effects=True, vmem_limit_bytes=56 * 1024 * 1024
@@ -644,7 +628,7 @@
         out_shape=(result, result),
         in_specs=[vmem_spec] * 2,
         out_specs=(any_spec, any_spec),
-        scratch_shapes=[dma((2, 4 if local % 64 == 0 else 1))],
+        scratch_shapes=[dma((2,))],
         compiler_params=pltpu.CompilerParams(vmem_limit_bytes=2 * 1024 * 1024),
     )(layer_output, tokens_grad)
 

time: 26.7 us -> 26.3 us (0.985)
  no operation moved by 1% of the time
where the time goes in v3:
time: 26.3 us; the launch traced here: 26.1 us
  Pallas kernels  25.5 us (97%)
  between operations  0.64 us (2%)
    pallas_call x1, Pallas kernels, on_device(): pl.pallas_call(functools.partial(kernel, n_ctx, n_tp, reach, per_kv, kv_c...  24.4 us
    pallas_call x1, Pallas kernels, on_device(): pl.pallas_call(write, out_shape=(result, result), in_specs=[vmem_spec] *...  1.08 us

profile of v3, /device:TPU:0, one launch (start us, length us, event | category | flops | bytes accessed | tf_op | source)
XLA Modules:
  0.0 26.1 jit_solution(16423433391430909181)
XLA Ops:
  0.6 24.4 %shard_map.104 = (bf16[128,2688]{1,0:T(8,128)(2,1)S(1)}, bf16[128,2688]{1,0:T(8,128)(2,1)S(1)}) custom-call(bf16[128,2688]{1,0:T(8,128)(2,1)} %tokens.1, bf16[128,2688]{1,0:T(8,128)(2,1)} %rgrad.1, bf16[2688,256]{1,0:T(8,128)(2,1)} %qw.1, bf16[2688,128]{1,0:T(8,128)(2,1)} %kw.1, bf16[2688,128]{1,0:T(8,128)(2,1)} %vw.1, bf16[256,2688]{1,0:T(8,128)(2,1)} %ow.1, ...), custom_call_target="tpu_custom_call" | custom-call | tf_op jit(solution)/shard_map/pallas_call | solution.py:576
  25.0 1.1 %shard_map.105 = (bf16[128,2688]{1,0:T(8,128)(2,1)}, bf16[128,2688]{1,0:T(8,128)(2,1)}) custom-call(bf16[128,2688]{1,0:T(8,128)(2,1)S(1)} %get-tuple-element.4.a, bf16[128,2688]{1,0:T(8,128)(2,1)S(1)} %get-tuple-element.5.b), custom_call_target="tpu_custom_call" | custom-call | tf_op jit(solution)/shard_map/pallas_call | solution.py:626

commit v4 on v3

--- a/solution.py
+++ b/solution.py
@@ -504,18 +504,15 @@
         for n, (lo, hi) in enumerate(tiles):
             piece = product(back[span, qc:], n, qc, qc + 2 * kc, False)
             if w == 0:
-                acc[1, :, lo:hi] += piece
+                total = acc[1, :, lo:hi] + piece
+                for j in range(1, n_tp):
+                    rs_copy(2, j, n).wait_recv()
+                    total += rs_in[2, j - 1, :, lo:hi].astype(f32)
+                gout_ref[:, lo:hi] = total.astype(bf16)
             else:
                 for j in range(1, n_tp):
                     part[2, j, :, lo:hi] = piece[(j - 1) * local : j * local].astype(bf16)
                     rs_copy(2, j, n).start()
-    for n, (lo, hi) in enumerate(tiles):
-        total = acc[1, :, lo:hi]
-        for j in range(1, n_tp):
-            rs_copy(2, j, n).wait_recv()
-            total += rs_in[2, j - 1, :, lo:hi].astype(f32)
-        gout_ref[:, lo:hi] = total.astype(bf16)
-
     def sent(sem, ref):
         pltpu.make_async_copy(ref, ref, sem).wait()
 

time: 26.3 us -> 26.3 us (level)
  no operation moved by 1% of the time
where the time goes in v4:
time: 26.3 us; the launch traced here: 26.2 us
  Pallas kernels  25.5 us (97%)
  between operations  0.64 us (2%)
    pallas_call x1, Pallas kernels, on_device(): pl.pallas_call(functools.partial(kernel, n_ctx, n_tp, reach, per_kv, kv_c...  24.5 us
    pallas_call x1, Pallas kernels, on_device(): pl.pallas_call(write, out_shape=(result, result), in_specs=[vmem_spec] *...  1.08 us

profile of v4, /device:TPU:0, one launch (start us, length us, event | category | flops | bytes accessed | tf_op | source)
XLA Modules:
  0.0 26.2 jit_solution(9930812350961729076)
XLA Ops:
  0.6 24.5 %shard_map.104 = (bf16[128,2688]{1,0:T(8,128)(2,1)S(1)}, bf16[128,2688]{1,0:T(8,128)(2,1)S(1)}) custom-call(bf16[128,2688]{1,0:T(8,128)(2,1)} %tokens.1, bf16[128,2688]{1,0:T(8,128)(2,1)} %rgrad.1, bf16[2688,256]{1,0:T(8,128)(2,1)} %qw.1, bf16[2688,128]{1,0:T(8,128)(2,1)} %kw.1, bf16[2688,128]{1,0:T(8,128)(2,1)} %vw.1, bf16[256,2688]{1,0:T(8,128)(2,1)} %ow.1, ...), custom_call_target="tpu_custom_call" | custom-call | tf_op jit(solution)/shard_map/pallas_call | solution.py:573
  25.1 1.1 %shard_map.105 = (bf16[128,2688]{1,0:T(8,128)(2,1)}, bf16[128,2688]{1,0:T(8,128)(2,1)}) custom-call(bf16[128,2688]{1,0:T(8,128)(2,1)S(1)} %get-tuple-element.4.a, bf16[128,2688]{1,0:T(8,128)(2,1)S(1)} %get-tuple-element.5.b), custom_call_target="tpu_custom_call" | custom-call | tf_op jit(solution)/shard_map/pallas_call | solution.py:623
